TPU v7x, 32 devices: a whole 2x2x4 slice. The times are simulated.
32 devices in a mesh: batch: 4 (over y, x), seq: 8 (over z, core).
Axes of the slice: x: 2, y: 2, z: 4, core: 2. Of those that a mesh axis runs over, the one named last changes fastest.
Arguments:
- inputs: bfloat16 [2, 4, 1024, 1024], P(None, 'batch', 'seq'), may hold values from -6 to 6
- w_query: bfloat16 [1024, 1024], P('seq'), may hold values from -0.1875 to 0.1875
- w_key: bfloat16 [1024, 1024], P('seq'), may hold values from -0.1875 to 0.1875
- w_value: bfloat16 [1024, 1024], P('seq'), may hold values from -0.1875 to 0.1875
- w_output: bfloat16 [1024, 1024], P('seq'), may hold values from -0.75 to 0.75
- gain_attention: bfloat16 [1024], P('seq'), may hold values from 0.25 to 1.75
- w_gate: bfloat16 [1024, 4096], P('seq'), may hold values from -0.1875 to 0.1875
- w_up: bfloat16 [1024, 4096], P('seq'), may hold values from -0.1875 to 0.1875
- w_down: bfloat16 [4096, 1024], P('seq'), may hold values from -0.1875 to 0.1875
- gain_feed: bfloat16 [1024], P('seq'), may hold values from 0.25 to 1.75
- variate_bias: float32 [2, 16], replicated, may hold values from -1 to 1
- segment_ids: int32 [2, 4, 1024], P(None, 'batch', 'seq'), may hold values from 0 to 1, never falling along the last dimension, each value on 1 to 768 neighbouring positions
- variate_ids: int32 [2, 4, 1024], P(None, 'batch', 'seq'), may hold values from 0 to 3
- positions: int32 [2, 4, 1024], P(None, 'batch', 'seq'), may hold values from 0 to 1023
- grad_output: bfloat16 [2, 4, 1024, 1024], P(None, 'batch', 'seq'), may hold values from -6 to 6
Outputs:
- block_output: bfloat16 [2, 4, 1024, 1024], P(None, 'batch', 'seq')
- grad_inputs: float32 [2, 4, 1024, 1024], P(None, 'batch', 'seq')
- grad_w_query: float32 [1024, 1024], P('seq')
- grad_w_key: float32 [1024, 1024], P('seq')
- grad_w_value: float32 [1024, 1024], P('seq')
- grad_w_output: float32 [1024, 1024], P('seq')
- grad_gain_attention: float32 [1024], P('seq')
- grad_w_gate: float32 [1024, 4096], P('seq')
- grad_w_up: float32 [1024, 4096], P('seq')
- grad_w_down: float32 [4096, 1024], P('seq')
- grad_gain_feed: float32 [1024], P('seq')
- grad_variate_bias: float32 [2, 16], replicated
Inputs may be any that keep to these rules, and one draw needn't show every extreme that they name: `segment_ids`: segment numbers never fall along a sequence; a document has 1 to 768 tokens.
All inputs are finite; a program needn't handle non-finite values.
Results may differ from a plain program's by a relative error of at most 0.038.
Values may be sent and summed in bfloat16 or wider, within the bound.
No kernel may reach another device: no remote copies, remote signals or barrier semaphores. Data moves between devices by JAX's collectives and lax.ppermute only.
A program may use at most 320 MiB of HBM per device.

v0:
```python
import math

import jax
import jax.numpy as jnp
from jax import lax
from jax.sharding import PartitionSpec as P

D = 1024
H = 16
HD = 64
REACH = 6


EPSILON = 1e-05
SCORE_SCALE = 0.125
MASKED = -1e30


def from_behind(value, axis, by):
    length = lax.axis_size(axis)
    pairs = [(i, i + by) for i in range(length) if 0 <= i + by < length]
    return lax.ppermute(value, axis, pairs)


def step_offset(step):
    distance = step // 2 + 1
    return distance if step % 2 == 0 else -distance


def rotary(values_in, positions_in, turn):
    row_count = values_in.shape[0]
    halfway = HD // 2
    freqs = jnp.exp(jnp.arange(halfway, dtype=jnp.float32) * (-2.0 * math.log(10000.0) / HD))
    angles = positions_in.astype(jnp.float32)[:, None] * freqs[None, :]
    cosine = jnp.cos(angles)[:, None, :]
    sine = turn * jnp.sin(angles)[:, None, :]
    shaped = values_in.reshape(row_count, H, HD)
    first_half = shaped[..., :halfway]
    second_half = shaped[..., halfway:]
    turned = jnp.concatenate(
        [first_half * cosine - second_half * sine, first_half * sine + second_half * cosine], -1
    )
    return turned.reshape(row_count, H * HD)


def head_scores(query_heads, key_heads, query_variates, key_variates, bias_table):
    raw = jnp.einsum("qhd,khd->hqk", query_heads, key_heads, preferred_element_type=jnp.float32)
    same_variate = (query_variates[:, None] == key_variates[None, :])[None]
    return raw * SCORE_SCALE + jnp.where(
        same_variate, bias_table[0][:, None, None], bias_table[1][:, None, None]
    )


def attend_forward(query_rows, own_keys, own_values, own_segments, own_variates, bias_table):
    tok_count = query_rows.shape[0]
    query_heads = query_rows.reshape(tok_count, H, HD)
    shifted_segments = own_segments + 1

    def fold_keys(carried, piece_rows):
        key_part, value_part, segment_part, variate_part = piece_rows
        part_count = key_part.shape[0]
        live = shifted_segments[:, None] == segment_part[None, :]

        def update(state):
            running_max, running_total, running_sum = state
            logits = head_scores(
                query_heads,
                key_part.reshape(part_count, H, HD),
                own_variates,
                variate_part,
                bias_table,
            )
            logits = jnp.where(live[None], logits, MASKED)
            new_max = jnp.maximum(running_max, jnp.max(logits, -1))
            rescale = jnp.exp(running_max - new_max)
            weights = jnp.where(live[None], jnp.exp(logits - new_max[..., None]), 0.0)
            new_total = running_total * rescale + jnp.sum(weights, -1)
            mixed = jnp.einsum(
                "hqk,khd->qhd",
                weights.astype(jnp.bfloat16),
                value_part.reshape(part_count, H, HD),
                preferred_element_type=jnp.float32,
            )
            new_sum = running_sum * jnp.transpose(rescale)[:, :, None] + mixed
            return (new_max, new_total, new_sum)

        return lax.cond(jnp.any(live), update, lambda state: state, carried)

    near_rows = (own_keys, own_values, shifted_segments, own_variates)
    state = (
        jnp.full((H, tok_count), MASKED, jnp.float32),
        jnp.zeros((H, tok_count), jnp.float32),
        jnp.zeros((tok_count, H, HD), jnp.float32),
    )
    state = fold_keys(state, near_rows)
    for step in range(2 * REACH):
        arrived = from_behind(
            (own_keys, own_values, shifted_segments, own_variates), "seq", step_offset(step)
        )
        state = fold_keys(state, arrived)
    final_max, final_total, final_sum = state
    attended = final_sum / jnp.transpose(final_total)[:, :, None]
    log_rows = jnp.transpose(final_max + jnp.log(final_total))
    return (attended.reshape(tok_count, H * HD), log_rows)


def attend_queries_back(
    query_rows,
    grad_rows,
    log_rows,
    delta_rows,
    own_keys,
    own_values,
    own_segments,
    own_variates,
    bias_table,
):
    tok_count = query_rows.shape[0]
    query_heads = query_rows.reshape(tok_count, H, HD)
    grad_heads = grad_rows.reshape(tok_count, H, HD)
    log_heads = jnp.transpose(log_rows)
    delta_heads = jnp.transpose(delta_rows)
    shifted_segments = own_segments + 1

    def fold_keys_back(carried, piece_rows):
        key_part, value_part, segment_part, variate_part = piece_rows
        part_count = key_part.shape[0]
        live = shifted_segments[:, None] == segment_part[None, :]

        def update(state):
            grad_query, grad_bias = state
            key_heads = key_part.reshape(part_count, H, HD)
            logits = head_scores(query_heads, key_heads, own_variates, variate_part, bias_table)
            weights = jnp.where(live[None], jnp.exp(logits - log_heads[..., None]), 0.0)
            grad_weights = jnp.einsum(
                "qhd,khd->hqk",
                grad_heads,
                value_part.reshape(part_count, H, HD),
                preferred_element_type=jnp.float32,
            )
            grad_logits = (weights * (grad_weights - delta_heads[..., None])).astype(jnp.bfloat16)
            grad_query = grad_query + SCORE_SCALE * jnp.einsum(
                "hqk,khd->qhd", grad_logits, key_heads, preferred_element_type=jnp.float32
            )
            same_variate = (own_variates[:, None] == variate_part[None, :])[None]
            logit_values = grad_logits.astype(jnp.float32)
            same_total = jnp.sum(jnp.where(same_variate, logit_values, 0.0), axis=(1, 2))
            other_total = jnp.sum(jnp.where(same_variate, 0.0, logit_values), axis=(1, 2))
            return (grad_query, grad_bias + jnp.stack([same_total, other_total]))

        return lax.cond(jnp.any(live), update, lambda state: state, carried)

    state = (jnp.zeros((tok_count, H, HD), jnp.float32), jnp.zeros((2, H), jnp.float32))
    state = fold_keys_back(state, (own_keys, own_values, shifted_segments, own_variates))
    for step in range(2 * REACH):
        arrived = from_behind(
            (own_keys, own_values, shifted_segments, own_variates), "seq", step_offset(step)
        )
        state = fold_keys_back(state, arrived)
    grad_query, grad_bias = state
    return (grad_query.reshape(tok_count, H * HD), grad_bias)


def attend_keys_back(
    query_rows,
    grad_rows,
    log_rows,
    delta_rows,
    own_keys,
    own_values,
    own_segments,
    own_variates,
    bias_table,
):
    tok_count = own_keys.shape[0]
    key_heads = own_keys.reshape(tok_count, H, HD)
    value_heads = own_values.reshape(tok_count, H, HD)
    shifted_segments = own_segments + 1

    def fold_queries(carried, piece_rows):
        query_part, grad_part, log_part, delta_part, segment_part, variate_part = piece_rows
        part_count = query_part.shape[0]
        live = segment_part[:, None] == shifted_segments[None, :]

        def update(state):
            grad_key, grad_value = state
            query_heads = query_part.reshape(part_count, H, HD)
            grad_heads = grad_part.reshape(part_count, H, HD)
            logits = head_scores(query_heads, key_heads, variate_part, own_variates, bias_table)
            weights = jnp.where(
                live[None], jnp.exp(logits - jnp.transpose(log_part)[..., None]), 0.0
            )
            grad_value = grad_value + jnp.einsum(
                "hqk,qhd->khd",
                weights.astype(jnp.bfloat16),
                grad_heads,
                preferred_element_type=jnp.float32,
            )
            grad_weights = jnp.einsum(
                "qhd,khd->hqk", grad_heads, value_heads, preferred_element_type=jnp.float32
            )
            grad_logits = (weights * (grad_weights - jnp.transpose(delta_part)[..., None])).astype(
                jnp.bfloat16
            )
            grad_key = grad_key + SCORE_SCALE * jnp.einsum(
                "hqk,qhd->khd", grad_logits, query_heads, preferred_element_type=jnp.float32
            )
            return (grad_key, grad_value)

        return lax.cond(jnp.any(live), update, lambda state: state, carried)

    state = (jnp.zeros((tok_count, H, HD), jnp.float32), jnp.zeros((tok_count, H, HD), jnp.float32))
    state = fold_queries(
        state, (query_rows, grad_rows, log_rows, delta_rows, shifted_segments, own_variates)
    )
    for step in range(2 * REACH):
        arrived = (
            from_behind(query_rows, "seq", step_offset(step)),
            from_behind(grad_rows, "seq", step_offset(step)),
            from_behind(log_rows.astype(jnp.bfloat16), "seq", step_offset(step)).astype(
                log_rows.dtype
            ),
            from_behind(delta_rows.astype(jnp.bfloat16), "seq", step_offset(step)).astype(
                delta_rows.dtype
            ),
            from_behind(shifted_segments, "seq", step_offset(step)),
            from_behind(own_variates, "seq", step_offset(step)),
        )
        state = fold_queries(state, arrived)
    grad_key, grad_value = state
    return (grad_key.reshape(tok_count, H * HD), grad_value.reshape(tok_count, H * HD))


def norm_back(grad_normed, normed, scale_rows):
    return scale_rows * (grad_normed - normed * jnp.mean(grad_normed * normed, -1, keepdims=True))


def on_device(
    inputs,
    w_query,
    w_key,
    w_value,
    w_output,
    gain_attention,
    w_gate,
    w_up,
    w_down,
    gain_feed,
    variate_bias,
    segment_ids,
    variate_ids,
    positions,
    grad_output,
):
    micro_count = inputs.shape[0]
    tok_count = inputs.shape[2]
    row_count = micro_count * tok_count
    residual_in = inputs.reshape(row_count, D).astype(jnp.float32)
    cotangent = grad_output.reshape(row_count, D).astype(jnp.float32)
    segment_rows = segment_ids.reshape(micro_count, tok_count)
    variate_rows = variate_ids.reshape(micro_count, tok_count)
    position_rows = positions.reshape(row_count)
    full_query, full_key, full_value, full_output, full_gain_first = (
        lax.all_gather(w_query, "seq", axis=0, tiled=True),
        lax.all_gather(w_key, "seq", axis=0, tiled=True),
        lax.all_gather(w_value, "seq", axis=0, tiled=True),
        lax.all_gather(w_output, "seq", axis=0, tiled=True),
        lax.all_gather(gain_attention, "seq", axis=0, tiled=True),
    )
    full_gate, full_up, full_down, full_gain_second = (
        lax.all_gather(w_gate, "seq", axis=0, tiled=True),
        lax.all_gather(w_up, "seq", axis=0, tiled=True),
        lax.all_gather(w_down, "seq", axis=0, tiled=True),
        lax.all_gather(gain_feed, "seq", axis=0, tiled=True),
    )
    scale_first = lax.rsqrt(jnp.mean(residual_in * residual_in, -1, keepdims=True) + EPSILON)
    normed_first = residual_in * scale_first
    mixed_first = (normed_first * full_gain_first.astype(jnp.float32)).astype(jnp.bfloat16)
    query_proj = jnp.dot(mixed_first, full_query, preferred_element_type=jnp.float32)
    key_proj = jnp.dot(mixed_first, full_key, preferred_element_type=jnp.float32)
    value_proj = jnp.dot(mixed_first, full_value, preferred_element_type=jnp.float32)
    query_rows = rotary(query_proj, position_rows, 1.0).astype(jnp.bfloat16)
    key_rows = rotary(key_proj, position_rows, 1.0).astype(jnp.bfloat16)
    value_rows = value_proj.astype(jnp.bfloat16)
    attended_parts = []
    log_parts = []
    for micro_index in range(micro_count):
        lower_row = micro_index * tok_count
        upper_row = lower_row + tok_count
        attended_part, log_part = attend_forward(
            query_rows[lower_row:upper_row],
            key_rows[lower_row:upper_row],
            value_rows[lower_row:upper_row],
            segment_rows[micro_index],
            variate_rows[micro_index],
            variate_bias,
        )
        attended_parts.append(attended_part)
        log_parts.append(log_part)
    attended_all = jnp.concatenate(attended_parts, 0)
    attended_low = attended_all.astype(jnp.bfloat16)
    middle = residual_in + jnp.dot(attended_low, full_output, preferred_element_type=jnp.float32)
    scale_second = lax.rsqrt(jnp.mean(middle * middle, -1, keepdims=True) + EPSILON)
    normed_second = middle * scale_second
    mixed_second = (normed_second * full_gain_second.astype(jnp.float32)).astype(jnp.bfloat16)
    gate_proj = jnp.dot(mixed_second, full_gate, preferred_element_type=jnp.float32)
    up_proj = jnp.dot(mixed_second, full_up, preferred_element_type=jnp.float32)
    sigmoid_gate = jax.nn.sigmoid(gate_proj)
    silu_gate = gate_proj * sigmoid_gate
    hidden_rows = (silu_gate * up_proj).astype(jnp.bfloat16)
    block_rows = middle + jnp.dot(hidden_rows, full_down, preferred_element_type=jnp.float32)
    block_output = block_rows.astype(jnp.bfloat16).reshape(inputs.shape)
    full_query, full_key, full_value, full_output, full_gain_first = (
        lax.all_gather(w_query, "seq", axis=0, tiled=True),
        lax.all_gather(w_key, "seq", axis=0, tiled=True),
        lax.all_gather(w_value, "seq", axis=0, tiled=True),
        lax.all_gather(w_output, "seq", axis=0, tiled=True),
        lax.all_gather(gain_attention, "seq", axis=0, tiled=True),
    )
    full_gate, full_up, full_down, full_gain_second = (
        lax.all_gather(w_gate, "seq", axis=0, tiled=True),
        lax.all_gather(w_up, "seq", axis=0, tiled=True),
        lax.all_gather(w_down, "seq", axis=0, tiled=True),
        lax.all_gather(gain_feed, "seq", axis=0, tiled=True),
    )
    grad_branch_second = cotangent.astype(jnp.bfloat16)
    grad_down = jnp.einsum(
        "rf,rd->fd", hidden_rows, grad_branch_second, preferred_element_type=jnp.float32
    )
    grad_hidden = jnp.einsum(
        "rd,fd->rf", grad_branch_second, full_down, preferred_element_type=jnp.float32
    )
    silu_slope = sigmoid_gate * (1.0 + gate_proj * (1.0 - sigmoid_gate))
    grad_gate_rows = (grad_hidden * up_proj * silu_slope).astype(jnp.bfloat16)
    grad_up_rows = (grad_hidden * silu_gate).astype(jnp.bfloat16)
    grad_gate = jnp.einsum(
        "rd,rf->df", mixed_second, grad_gate_rows, preferred_element_type=jnp.float32
    )
    grad_up = jnp.einsum(
        "rd,rf->df", mixed_second, grad_up_rows, preferred_element_type=jnp.float32
    )
    grad_mixed_second = jnp.einsum(
        "rf,df->rd", grad_gate_rows, full_gate, preferred_element_type=jnp.float32
    ) + jnp.einsum("rf,df->rd", grad_up_rows, full_up, preferred_element_type=jnp.float32)
    grad_gain_second = jnp.sum(grad_mixed_second * normed_second, 0)
    grad_middle = cotangent + norm_back(
        grad_mixed_second * full_gain_second.astype(jnp.float32), normed_second, scale_second
    )
    grad_branch_first = grad_middle.astype(jnp.bfloat16)
    grad_out_proj = jnp.einsum(
        "rd,re->de", attended_low, grad_branch_first, preferred_element_type=jnp.float32
    )
    grad_attended = jnp.einsum(
        "re,de->rd", grad_branch_first, full_output, preferred_element_type=jnp.float32
    ).astype(jnp.bfloat16)
    delta_all = jnp.einsum(
        "rhd,rhd->rh",
        grad_attended.astype(jnp.float32).reshape(row_count, H, HD),
        attended_all.reshape(row_count, H, HD),
    )
    grad_bias_local = jnp.zeros((2, H), jnp.float32)
    query_grad_parts = []
    key_grad_parts = []
    value_grad_parts = []
    for micro_index in range(micro_count):
        lower_row = micro_index * tok_count
        upper_row = lower_row + tok_count
        query_grad_part, bias_part = attend_queries_back(
            query_rows[lower_row:upper_row],
            grad_attended[lower_row:upper_row],
            log_parts[micro_index],
            delta_all[lower_row:upper_row],
            key_rows[lower_row:upper_row],
            value_rows[lower_row:upper_row],
            segment_rows[micro_index],
            variate_rows[micro_index],
            variate_bias,
        )
        key_grad_part, value_grad_part = attend_keys_back(
            query_rows[lower_row:upper_row],
            grad_attended[lower_row:upper_row],
            log_parts[micro_index],
            delta_all[lower_row:upper_row],
            key_rows[lower_row:upper_row],
            value_rows[lower_row:upper_row],
            segment_rows[micro_index],
            variate_rows[micro_index],
            variate_bias,
        )
        grad_bias_local = grad_bias_local + bias_part
        query_grad_parts.append(query_grad_part)
        key_grad_parts.append(key_grad_part)
        value_grad_parts.append(value_grad_part)
    grad_query_rows = rotary(jnp.concatenate(query_grad_parts, 0), position_rows, -1.0).astype(
        jnp.bfloat16
    )
    grad_key_rows = rotary(jnp.concatenate(key_grad_parts, 0), position_rows, -1.0).astype(
        jnp.bfloat16
    )
    grad_value_rows = jnp.concatenate(value_grad_parts, 0).astype(jnp.bfloat16)
    grad_query = jnp.einsum(
        "rd,re->de", mixed_first, grad_query_rows, preferred_element_type=jnp.float32
    )
    grad_key = jnp.einsum(
        "rd,re->de", mixed_first, grad_key_rows, preferred_element_type=jnp.float32
    )
    grad_value = jnp.einsum(
        "rd,re->de", mixed_first, grad_value_rows, preferred_element_type=jnp.float32
    )
    grad_mixed_first = (
        jnp.einsum("re,de->rd", grad_query_rows, full_query, preferred_element_type=jnp.float32)
        + jnp.einsum("re,de->rd", grad_key_rows, full_key, preferred_element_type=jnp.float32)
        + jnp.einsum("re,de->rd", grad_value_rows, full_value, preferred_element_type=jnp.float32)
    )
    grad_gain_first = jnp.sum(grad_mixed_first * normed_first, 0)
    grad_input_rows = grad_middle + norm_back(
        grad_mixed_first * full_gain_first.astype(jnp.float32), normed_first, scale_first
    )
    grad_inputs = grad_input_rows.reshape(inputs.shape)
    (
        shard_query,
        shard_key,
        shard_value,
        shard_output,
        shard_gain_first,
        shard_gate,
        shard_up,
        shard_down,
        shard_gain_second,
    ) = (
        lax.psum_scatter(grad_query, "seq", scatter_dimension=0, tiled=True),
        lax.psum_scatter(grad_key, "seq", scatter_dimension=0, tiled=True),
        lax.psum_scatter(grad_value, "seq", scatter_dimension=0, tiled=True),
        lax.psum_scatter(grad_out_proj, "seq", scatter_dimension=0, tiled=True),
        lax.psum_scatter(grad_gain_first, "seq", scatter_dimension=0, tiled=True),
        lax.psum_scatter(grad_gate, "seq", scatter_dimension=0, tiled=True),
        lax.psum_scatter(grad_up, "seq", scatter_dimension=0, tiled=True),
        lax.psum_scatter(grad_down, "seq", scatter_dimension=0, tiled=True),
        lax.psum_scatter(grad_gain_second, "seq", scatter_dimension=0, tiled=True),
    )
    summed = (
        lax.psum(shard_query.astype(jnp.bfloat16), "batch").astype(jnp.float32),
        lax.psum(shard_key.astype(jnp.bfloat16), "batch").astype(jnp.float32),
        lax.psum(shard_value.astype(jnp.bfloat16), "batch").astype(jnp.float32),
        lax.psum(shard_output.astype(jnp.bfloat16), "batch").astype(jnp.float32),
        lax.psum(shard_gain_first.astype(jnp.bfloat16), "batch").astype(jnp.float32),
        lax.psum(shard_gate.astype(jnp.bfloat16), "batch").astype(jnp.float32),
        lax.psum(shard_up.astype(jnp.bfloat16), "batch").astype(jnp.float32),
        lax.psum(shard_down.astype(jnp.bfloat16), "batch").astype(jnp.float32),
        lax.psum(shard_gain_second.astype(jnp.bfloat16), "batch").astype(jnp.float32),
    )
    grad_bias_total = lax.psum(grad_bias_local, ("batch", "seq"))
    return (
        block_output,
        grad_inputs,
        summed[0],
        summed[1],
        summed[2],
        summed[3],
        summed[4],
        summed[5],
        summed[6],
        summed[7],
        summed[8],
        grad_bias_total,
    )


def solution(mesh):
    return jax.shard_map(
        on_device,
        mesh=mesh,
        in_specs=(
            P(None, "batch", "seq", None),
            P("seq", None),
            P("seq", None),
            P("seq", None),
            P("seq", None),
            P("seq"),
            P("seq", None),
            P("seq", None),
            P("seq", None),
            P("seq"),
            P(),
            P(None, "batch", "seq"),
            P(None, "batch", "seq"),
            P(None, "batch", "seq"),
            P(None, "batch", "seq", None),
        ),
        out_specs=(
            P(None, "batch", "seq", None),
            P(None, "batch", "seq", None),
            P("seq", None),
            P("seq", None),
            P("seq", None),
            P("seq", None),
            P("seq"),
            P("seq", None),
            P("seq", None),
            P("seq", None),
            P("seq"),
            P(),
        ),
        check_vma=False,
    )
```

profile of v0, /device:TPU:0, one launch (start us, length us, event | category | flops | bytes accessed | tf_op | source)
XLA Modules:
  0.0 2151.3 jit_solution(13253497317220967286)
XLA Ops:
  12.0 13.5 all-gather
  27.7 13.8 all-gather.10.cloned.1.call-done
  44.3 27.4 %all-gather.12.cloned.1.call-done = bf16[1024,1024]{1,0:T(8,128)(2,1)} async-done(((bf16[128,1024]{1,0:T(8,128)(2,1)}), bf16[1024,1024]{1,0:T(8,128)(2,1)}) %all-gather.12.cloned.1.call-update) | async-done | bytes 2097168 | tf_op jit(solution)/shard_map/all_gather | solution.py:264
  83.5 21.3 all-gather.14.cloned.1.call-done
  321.9 31.8 %collective-permute-start.36 = (bf16[128,1024]{0,1:T(8,128)(2,1)S(1)}, bf16[128,1024]{0,1:T(8,128)(2,1)S(1)}, u32[]{:S(2)}, u32[]{:S(2)}) collective-permute-start(bf16[128,1024]{0,1:T(8,128)(2,1)S(1)} %bitcast.1748), channel_id=1, source_target_pairs={{0,5},{1,6},{2,7},{8,13},{9,14},{10,15},{16,21},{17,22},{18,23},{2... | collective-permute-start | bytes 786440 | tf_op jit(solution)/shard_map/ppermute | solution.py:22
  357.7 53.1 %collective-permute-start.42 = (bf16[128,1024]{0,1:T(8,128)(2,1)S(1)}, bf16[128,1024]{0,1:T(8,128)(2,1)S(1)}, u32[]{:S(2)}, u32[]{:S(2)}) collective-permute-start(bf16[128,1024]{0,1:T(8,128)(2,1)S(1)} %bitcast.1750), channel_id=1, source_target_pairs={{0,6},{1,7},{8,14},{9,15},{16,22},{17,23},{24,30},{25,31}} | collective-permute-start | bytes 786440 | tf_op jit(solution)/shard_map/ppermute | solution.py:22
  414.9 15.6 collective-permute-done.41
  434.5 8.9 collective-permute-start.62
  481.6 19.0 collective-permute-start.84
  503.3 26.3 %all-gather.1 = bf16[8,1,128]{2,1,0:T(2,128)(2,1)S(1)} all-gather(bf16[1,1,128]{2,1,0:T(2,128)(2,1)S(1)} %bitcast.2035), channel_id=1, replica_groups=mesh['batch'=4,'seq'=8] {'seq'}, dimensions={0}, use_global_device_ids=true | all-gather | bytes 2304 | tf_op jit(solution)/shard_map/all_gather | solution.py:274
  659.6 12.4 multiply_convert_fusion
  693.7 24.3 %collective-permute-start.152 = (bf16[128,1024]{0,1:T(8,128)(2,1)S(1)}, bf16[128,1024]{0,1:T(8,128)(2,1)}, u32[]{:S(2)}, u32[]{:S(2)}) collective-permute-start(bf16[128,1024]{0,1:T(8,128)(2,1)S(1)} %bitcast.1759), channel_id=1, source_target_pairs={{0,2},{1,3},{2,4},{3,5},{4,6},{5,7},{8,10},{9,11},{10,12},{11,13},... | collective-permute-start | bytes 786440 | tf_op jit(solution)/shard_map/ppermute | solution.py:22
  750.8 26.1 %collective-permute-done.172 = bf16[128,1024]{0,1:T(8,128)(2,1)S(1)} collective-permute-done((bf16[128,1024]{0,1:T(8,128)(2,1)S(1)}, bf16[128,1024]{0,1:T(8,128)(2,1)S(1)}, u32[]{:S(2)}, u32[]{:S(2)}) %collective-permute-start.172) | collective-permute-done | bytes 262176 | tf_op jit(solution)/shard_map/ppermute | solution.py:22
  810.9 13.4 collective-permute-start.145
  825.6 10.3 collective-permute-done.124
  941.8 9.5 collective-permute-start.187
  981.7 10.1 collective-permute-start.139
  1003.6 10.2 collective-permute-start.170
  1021.0 13.2 collective-permute-start.186
  1065.0 16.9 collective-permute-start.136
  1338.0 9.7 fusion.984
  1347.8 9.8 fusion.985
  1358.7 9.8 fusion.986
  1372.2 95.3 %reduce-scatter.8.cloned.1.call-done = f32[128,1024]{1,0:T(8,128)} async-done(((f32[1024,1024]{1,0:T(8,128)}), f32[128,1024]{1,0:T(8,128)}) %reduce-scatter.8.cloned.1.call-update) | async-done | bytes 524304 | tf_op jit(solution)/shard_map/reduce_scatter | solution.py:431
  1469.2 48.7 %reduce-scatter.10.cloned.1.call-done = f32[128,1024]{1,0:T(8,128)} async-done(((f32[1024,1024]{1,0:T(8,128)}), f32[128,1024]{1,0:T(8,128)}) %reduce-scatter.10.cloned.1.call-update) | async-done | bytes 524304 | tf_op jit(solution)/shard_map/reduce_scatter | solution.py:432
  1519.7 166.9 %reduce-scatter.16.cloned.1.call-done = f32[128,4096]{1,0:T(8,128)} async-done(((f32[1024,4096]{1,0:T(8,128)}), f32[128,4096]{1,0:T(8,128)}) %reduce-scatter.16.cloned.1.call-update) | async-done | bytes 2097168 | tf_op jit(solution)/shard_map/reduce_scatter | solution.py:436
  1689.3 166.3 %reduce-scatter.18.cloned.1.call-done = f32[128,4096]{1,0:T(8,128)} async-done(((f32[1024,4096]{1,0:T(8,128)}), f32[128,4096]{1,0:T(8,128)}) %reduce-scatter.18.cloned.1.call-update) | async-done | bytes 2097168 | tf_op jit(solution)/shard_map/reduce_scatter | solution.py:437
  1858.2 166.1 %reduce-scatter.20.cloned.1.call-done = f32[512,1024]{1,0:T(8,128)} async-done(((f32[4096,1024]{1,0:T(8,128)}), f32[512,1024]{1,0:T(8,128)}) %reduce-scatter.20.cloned.1.call-update) | async-done | bytes 2097168 | tf_op jit(solution)/shard_map/reduce_scatter | solution.py:438
  2029.1 38.2 %psum.79 = f32[2,16]{1,0:T(2,128)} all-reduce(f32[2,16]{1,0:T(2,128)S(1)} %add.835), channel_id=1, replica_groups=mesh['batch'=4,'seq'=8] {'batch','seq'}, use_global_device_ids=true, to_apply=%region_334.335 | all-reduce | flops 32 | bytes 256 | tf_op jit(solution)/shard_map/psum | solution.py:452
  2079.1 15.7 all-reduce.2
  2095.0 9.8 all-reduce.3
  2107.0 28.2 %all-reduce.7.cloned.1.call-done = (bf16[128,1024]{1,0:T(8,128)(2,1)}, bf16[128,1024]{1,0:T(8,128)(2,1)}, bf16[128,1024]{1,0:T(8,128)(2,1)}, bf16[128,1024]{1,0:...) async-done(((bf16[128,1024]{1,0:T(8,128)(2,1)}, bf16[128,1024]{1,0:T(8,128)(2,1)}, bf16[128,1024]{1,0:T(8,128)(2,1)}, ...) | async-done | bytes 4194320 | tf_op jit(solution)/shard_map/psum | solution.py:442
  (1369 shorter events, 1168.8 us)
Async XLA Ops:
  7.9 63.8 %all-gather.12.cloned.1.call-start = ((), (), s32[]{:S(2)}) async-start(), calls=%async_computation.8 | async-start | bytes 2359296 | tf_op jit(solution)/shard_map/all_gather | solution.py:264
  8.7 96.1 %all-gather.14.cloned.1.call-start = ((), (), s32[]{:S(2)}) async-start(), calls=%async_computation.9 | async-start | bytes 2359296 | tf_op jit(solution)/shard_map/all_gather | solution.py:266
  9.4 631.5 %all-gather.16.cloned.1.call-start = ((), (), s32[]{:S(2)}) async-start(), calls=%async_computation.10 | async-start | bytes 2359296 | tf_op jit(solution)/shard_map/all_gather | solution.py:267
  10.0 633.7 %all-gather.18.cloned.1.call-start = ((), (), s32[]{:S(2)}) async-start(), calls=%async_computation.11 | async-start | bytes 9437184 | tf_op jit(solution)/shard_map/all_gather | solution.py:271
  10.6 641.2 %all-gather.20.cloned.1.call-start = ((), (), s32[]{:S(2)}) async-start(), calls=%async_computation.12 | async-start | bytes 9437184 | tf_op jit(solution)/shard_map/all_gather | solution.py:272
  11.2 648.5 %all-gather.22.cloned.1.call-start = ((), (), s32[]{:S(2)}) async-start(), calls=%async_computation.13 | async-start | bytes 9437184 | tf_op jit(solution)/shard_map/all_gather | solution.py:273
  11.9 1356.7 %reduce-scatter.14.cloned.1.call-start = ((), (), s32[]{:S(2)}) async-start(), calls=%async_computation.17 | async-start | bytes 4718592 | tf_op jit(solution)/shard_map/reduce_scatter | solution.py:434
  79.9 194.0 %collective-permute-start.12 = (bf16[128,1024]{0,1:T(8,128)(2,1)S(1)}, bf16[128,1024]{0,1:T(8,128)(2,1)S(1)}, u32[]{:S(2)}, u32[]{:S(2)}) collective-permute-start(bf16[128,1024]{0,1:T(8,128)(2,1)S(1)} %bitcast.1740), channel_id=1, source_target_pairs={{0,1},{1,2},{2,3},{3,4},{4,5},{5,6},{6,7},{8,9},{9,10},{10,11},{11... | collective-permute-start | bytes 786440 | tf_op jit(solution)/shard_map/ppermute | solution.py:22
  82.2 195.0 %collective-permute-start.15 = (bf16[128,1024]{0,1:T(8,128)(2,1)S(1)}, bf16[128,1024]{0,1:T(8,128)(2,1)}, u32[]{:S(2)}, u32[]{:S(2)}) collective-permute-start(bf16[128,1024]{0,1:T(8,128)(2,1)S(1)} %bitcast.1741), channel_id=1, source_target_pairs={{1,0},{2,1},{3,2},{4,3},{5,4},{6,5},{7,6},{9,8},{10,9},{11,10},{12... | collective-permute-start | bytes 786440 | tf_op jit(solution)/shard_map/ppermute | solution.py:22
  107.1 168.7 %collective-permute-start.14 = (bf16[128,1024]{1,0:T(8,128)(2,1)S(1)}, bf16[128,1024]{1,0:T(8,128)(2,1)S(1)}, u32[]{:S(2)}, u32[]{:S(2)}) collective-permute-start(bf16[128,1024]{1,0:T(8,128)(2,1)S(1)} %get-tuple-element.6508), channel_id=1, source_target_pairs={{0,1},{1,2},{2,3},{3,4},{4,5},{5,6},{6,7},{8,9},{9,10},{10,11},{11... | collective-permute-start | bytes 786440 | tf_op jit(solution)/shard_map/ppermute | solution.py:22
  321.9 89.0 %collective-permute-start.36 = (bf16[128,1024]{0,1:T(8,128)(2,1)S(1)}, bf16[128,1024]{0,1:T(8,128)(2,1)S(1)}, u32[]{:S(2)}, u32[]{:S(2)}) collective-permute-start(bf16[128,1024]{0,1:T(8,128)(2,1)S(1)} %bitcast.1748), channel_id=1, source_target_pairs={{0,5},{1,6},{2,7},{8,13},{9,14},{10,15},{16,21},{17,22},{18,23},{2... | collective-permute-start | bytes 786440 | tf_op jit(solution)/shard_map/ppermute | solution.py:22
  356.4 74.0 %collective-permute-start.41 = (bf16[128,1024]{1,0:T(8,128)(2,1)S(1)}, bf16[128,1024]{1,0:T(8,128)(2,1)S(1)}, u32[]{:S(2)}, u32[]{:S(2)}) collective-permute-start(bf16[128,1024]{1,0:T(8,128)(2,1)S(1)} %get-tuple-element.6508), channel_id=1, source_target_pairs={{5,0},{6,1},{7,2},{13,8},{14,9},{15,10},{21,16},{22,17},{23,18},{2... | collective-permute-start | bytes 786440 | tf_op jit(solution)/shard_map/ppermute | solution.py:22
  357.7 76.8 %collective-permute-start.42 = (bf16[128,1024]{0,1:T(8,128)(2,1)S(1)}, bf16[128,1024]{0,1:T(8,128)(2,1)S(1)}, u32[]{:S(2)}, u32[]{:S(2)}) collective-permute-start(bf16[128,1024]{0,1:T(8,128)(2,1)S(1)} %bitcast.1750), channel_id=1, source_target_pairs={{0,6},{1,7},{8,14},{9,15},{16,22},{17,23},{24,30},{25,31}} | collective-permute-start | bytes 786440 | tf_op jit(solution)/shard_map/ppermute | solution.py:22
  481.6 67.6 %collective-permute-start.84 = (bf16[128,1024]{0,1:T(8,128)(2,1)}, bf16[128,1024]{0,1:T(8,128)(2,1)}, u32[]{:S(2)}, u32[]{:S(2)}) collective-permute-start(bf16[128,1024]{0,1:T(8,128)(2,1)} %bitcast.631), channel_id=1, source_target_pairs={{0,5},{1,6},{2,7},{8,13},{9,14},{10,15},{16,21},{17,22},{18,23},{2... | collective-permute-start | bytes 786440 | tf_op jit(solution)/shard_map/ppermute | solution.py:22
  540.3 90.7 %collective-permute-start.89 = (bf16[128,1024]{1,0:T(8,128)(2,1)S(1)}, bf16[128,1024]{1,0:T(8,128)(2,1)}, u32[]{:S(2)}, u32[]{:S(2)}) collective-permute-start(bf16[128,1024]{1,0:T(8,128)(2,1)S(1)} %get-tuple-element.6509), channel_id=1, source_target_pairs={{5,0},{6,1},{7,2},{13,8},{14,9},{15,10},{21,16},{22,17},{23,18},{2... | collective-permute-start | bytes 786440 | tf_op jit(solution)/shard_map/ppermute | solution.py:22
  541.6 96.8 %collective-permute-start.90 = (bf16[128,1024]{0,1:T(8,128)(2,1)}, bf16[128,1024]{0,1:T(8,128)(2,1)}, u32[]{:S(2)}, u32[]{:S(2)}) collective-permute-start(bf16[128,1024]{0,1:T(8,128)(2,1)} %bitcast.631), channel_id=1, source_target_pairs={{0,6},{1,7},{8,14},{9,15},{16,22},{17,23},{24,30},{25,31}} | collective-permute-start | bytes 786440 | tf_op jit(solution)/shard_map/ppermute | solution.py:22
  549.2 89.2 %collective-permute-start.92 = (bf16[128,1024]{1,0:T(8,128)(2,1)S(1)}, bf16[128,1024]{1,0:T(8,128)(2,1)}, u32[]{:S(2)}, u32[]{:S(2)}) collective-permute-start(bf16[128,1024]{1,0:T(8,128)(2,1)S(1)} %get-tuple-element.6509), channel_id=1, source_target_pairs={{0,6},{1,7},{8,14},{9,15},{16,22},{17,23},{24,30},{25,31}} | collective-permute-start | bytes 786440 | tf_op jit(solution)/shard_map/ppermute | solution.py:22
  551.2 87.3 %collective-permute-start.93 = (bf16[128,1024]{0,1:T(8,128)(2,1)}, bf16[128,1024]{0,1:T(8,128)(2,1)}, u32[]{:S(2)}, u32[]{:S(2)}) collective-permute-start(bf16[128,1024]{0,1:T(8,128)(2,1)} %bitcast.631), channel_id=1, source_target_pairs={{6,0},{7,1},{14,8},{15,9},{22,16},{23,17},{30,24},{31,25}} | collective-permute-start | bytes 786440 | tf_op jit(solution)/shard_map/ppermute | solution.py:22
  552.5 86.0 %collective-permute-start.95 = (bf16[128,1024]{1,0:T(8,128)(2,1)S(1)}, bf16[128,1024]{1,0:T(8,128)(2,1)}, u32[]{:S(2)}, u32[]{:S(2)}) collective-permute-start(bf16[128,1024]{1,0:T(8,128)(2,1)S(1)} %get-tuple-element.6509), channel_id=1, source_target_pairs={{6,0},{7,1},{14,8},{15,9},{22,16},{23,17},{30,24},{31,25}} | collective-permute-start | bytes 786440 | tf_op jit(solution)/shard_map/ppermute | solution.py:22
  686.3 684.1 %reduce-scatter.12.cloned.1.call-start = ((), (), s32[]{:S(2)}) async-start(), calls=%async_computation.16 | async-start | bytes 4718592 | tf_op jit(solution)/shard_map/reduce_scatter | solution.py:433
  894.3 108.0 %collective-permute-start.146 = (bf16[128,1024]{1,0:T(8,128)(2,1)S(1)}, bf16[128,1024]{1,0:T(8,128)(2,1)S(1)}, u32[]{:S(2)}, u32[]{:S(2)}) collective-permute-start(bf16[128,1024]{1,0:T(8,128)(2,1)S(1)} %get-tuple-element.6506), channel_id=1, source_target_pairs={{0,1},{1,2},{2,3},{3,4},{4,5},{5,6},{6,7},{8,9},{9,10},{10,11},{11... | collective-permute-start | bytes 786440 | tf_op jit(solution)/shard_map/ppermute | solution.py:22
  1063.7 170.1 %collective-permute-start.134 = (bf16[128,1024]{1,0:T(8,128)(2,1)}, bf16[128,1024]{1,0:T(8,128)(2,1)}, u32[]{:S(2)}, u32[]{:S(2)}) collective-permute-start(bf16[128,1024]{1,0:T(8,128)(2,1)} %get-tuple-element.6507), channel_id=1, source_target_pairs={{5,0},{6,1},{7,2},{13,8},{14,9},{15,10},{21,16},{22,17},{23,18},{2... | collective-permute-start | bytes 786440 | tf_op jit(solution)/shard_map/ppermute | solution.py:22
  1065.0 169.8 %collective-permute-start.136 = (bf16[128,1024]{0,1:T(8,128)(2,1)}, bf16[128,1024]{0,1:T(8,128)(2,1)}, u32[]{:S(2)}, u32[]{:S(2)}) collective-permute-start(bf16[128,1024]{0,1:T(8,128)(2,1)} %bitcast.647), channel_id=1, source_target_pairs={{0,6},{1,7},{8,14},{9,15},{16,22},{17,23},{24,30},{25,31}} | collective-permute-start | bytes 786440 | tf_op jit(solution)/shard_map/ppermute | solution.py:22
  1081.9 152.8 %collective-permute-start.138 = (bf16[128,1024]{1,0:T(8,128)(2,1)}, bf16[128,1024]{1,0:T(8,128)(2,1)}, u32[]{:S(2)}, u32[]{:S(2)}) collective-permute-start(bf16[128,1024]{1,0:T(8,128)(2,1)} %get-tuple-element.6507), channel_id=1, source_target_pairs={{0,6},{1,7},{8,14},{9,15},{16,22},{17,23},{24,30},{25,31}} | collective-permute-start | bytes 786440 | tf_op jit(solution)/shard_map/ppermute | solution.py:22
  1085.8 149.9 %collective-permute-start.140 = (bf16[128,1024]{0,1:T(8,128)(2,1)}, bf16[128,1024]{0,1:T(8,128)(2,1)}, u32[]{:S(2)}, u32[]{:S(2)}) collective-permute-start(bf16[128,1024]{0,1:T(8,128)(2,1)} %bitcast.647), channel_id=1, source_target_pairs={{6,0},{7,1},{14,8},{15,9},{22,16},{23,17},{30,24},{31,25}} | collective-permute-start | bytes 786440 | tf_op jit(solution)/shard_map/ppermute | solution.py:22
  1087.1 148.6 %collective-permute-start.142 = (bf16[128,1024]{1,0:T(8,128)(2,1)}, bf16[128,1024]{1,0:T(8,128)(2,1)}, u32[]{:S(2)}, u32[]{:S(2)}) collective-permute-start(bf16[128,1024]{1,0:T(8,128)(2,1)} %get-tuple-element.6507), channel_id=1, source_target_pairs={{6,0},{7,1},{14,8},{15,9},{22,16},{23,17},{30,24},{31,25}} | collective-permute-start | bytes 786440 | tf_op jit(solution)/shard_map/ppermute | solution.py:22
  1240.9 226.6 %reduce-scatter.8.cloned.1.call-start = ((), (), s32[]{:S(2)}) async-start(), calls=%async_computation.14 | async-start | bytes 4718592 | tf_op jit(solution)/shard_map/reduce_scatter | solution.py:431
  1334.0 183.9 %reduce-scatter.10.cloned.1.call-start = ((), (), s32[]{:S(2)}) async-start(), calls=%async_computation.15 | async-start | bytes 4718592 | tf_op jit(solution)/shard_map/reduce_scatter | solution.py:432
  1337.0 349.6 %reduce-scatter.16.cloned.1.call-start = ((), (), s32[]{:S(2)}) async-start(), calls=%async_computation.18 | async-start | bytes 18874368 | tf_op jit(solution)/shard_map/reduce_scatter | solution.py:436
  1347.8 507.8 %reduce-scatter.18.cloned.1.call-start = ((), (), s32[]{:S(2)}) async-start(), calls=%async_computation.19 | async-start | bytes 18874368 | tf_op jit(solution)/shard_map/reduce_scatter | solution.py:437
  1357.7 666.7 %reduce-scatter.20.cloned.1.call-start = ((), (), s32[]{:S(2)}) async-start(), calls=%async_computation.20 | async-start | bytes 18874368 | tf_op jit(solution)/shard_map/reduce_scatter | solution.py:438
  1368.5 766.7 %all-reduce.7.cloned.1.call-start = ((), (), s32[]{:S(2)}) async-start(), calls=%async_computation.21 | async-start | bytes 8388608 | tf_op jit(solution)/shard_map/psum | solution.py:442
  (437 other events, 10274.3 us)
Sparse Core Ops, SparseCore 0:
  9.6 31.7 all-gather.9
  43.1 28.5 all-gather.11
  73.3 31.3 all-gather.13
  106.2 28.6 all-gather.15
  136.3 81.5 all-gather.17
  219.3 95.9 all-gather.19
  316.9 128.0 all-gather.21
  686.4 117.6 reduce-scatter.13
  1241.0 97.2 reduce-scatter.11
  1340.4 127.0 reduce-scatter.7
  1469.8 48.1 reduce-scatter.9
  1520.2 166.3 reduce-scatter.15
  1688.9 166.5 reduce-scatter.17
  1857.8 166.5 reduce-scatter.19
  2029.9 105.2 all-reduce.6
where the time goes:
time: 2150 us
  waiting for transfers between devices  841 us (39%)
  starting transfers between devices  702 us (33%)
  matrix products  238 us (11%)
  other arithmetic  129 us (6%)
  blocking collectives  103 us (5%)
  local copies, waits for them, and re-layouts  81.4 us (4%)
  between operations  51.8 us (2%)
    ppermute x192, starting transfers between devices, from_behind(): return lax.ppermute(value, axis, pairs)  702 us
    reduce_scatter x1, waiting for transfers between devices, on_device(): lax.psum_scatter(grad_gate, 'seq', scatter_dimension=0, tiled=True)  167 us
    reduce_scatter x1, waiting for transfers between devices, on_device(): lax.psum_scatter(grad_up, 'seq', scatter_dimension=0, tiled=True)  166 us
    reduce_scatter x1, waiting for transfers between devices, on_device(): lax.psum_scatter(grad_down, 'seq', scatter_dimension=0, tiled=True)  166 us
    ppermute x192, waiting for transfers between devices, from_behind(): return lax.ppermute(value, axis, pairs)  103 us
    reduce_scatter x1, waiting for transfers between devices, on_device(): lax.psum_scatter(grad_query, 'seq', scatter_dimension=0, tiled=True)  95.3 us
    dot_general x30, matrix products, head_scores(): jnp.einsum('qhd,khd->hqk', query_heads, key_heads, preferred_element_type...  65.8 us
    reduce_scatter x1, waiting for transfers between devices, on_device(): lax.psum_scatter(grad_key, 'seq', scatter_dimension=0, tiled=True)  48.7 us
  transfers between devices with their start and end apart: 207, of which 32 were waited for; matrix products, arithmetic and copies ran while one was open for 17% of the time, Pallas kernels for 0%

commit v1 on v0

--- a/solution.py
+++ b/solution.py
@@ -3,6 +3,8 @@
 import jax
 import jax.numpy as jnp
 from jax import lax
+from jax.experimental import pallas as pl
+from jax.experimental.pallas import tpu as pltpu
 from jax.sharding import PartitionSpec as P
 
 D = 1024
@@ -466,9 +468,566 @@
     )
 
 
+ORDER_A = (0, 1, 2, 3)
+ORDER_B = (0, 2, 1, 3)
+FEATURES = 128
+LSE_AT = 64
+
+
+def swap(value, bit):
+    return lax.ppermute(value, "batch", [(i, i ^ bit) for i in range(4)])
+
+
+def gather_plane(own):
+    half = own.shape[0] // 2
+    lower, upper = own[:half], own[half:]
+    lower_pair = jnp.concatenate([lower, swap(lower, 1)], 0)
+    upper_pair = jnp.concatenate([upper, swap(upper, 2)], 0)
+    return lower_pair, swap(lower_pair, 2), upper_pair, swap(upper_pair, 1)
+
+
+def scatter_plane(partial):
+    quarter = partial.shape[0] // 4
+    half = quarter // 2
+    lower = partial[:quarter] + swap(partial[quarter : 2 * quarter], 2)
+    upper = partial[2 * quarter : 3 * quarter] + swap(partial[3 * quarter :], 1)
+    return jnp.concatenate(
+        [lower[:half] + swap(lower[half:], 1), upper[:half] + swap(upper[half:], 2)], 0
+    )
+
+
+def by_rank(stacked, rank):
+    return jnp.stack([lax.dynamic_index_in_dim(stacked, rank ^ a, 0, False) for a in range(4)])
+
+
+def reorder(rows, order, mask):
+    blocks = rows.reshape(4, rows.shape[0] // 4, rows.shape[1])
+    return jnp.concatenate([blocks[order.index(r ^ mask)] for r in order], 0)
+
+
+def gather_heads(own):
+    half = own.shape[0] // 2
+    lower, upper = own[:half], own[half:]
+    lower_x = reorder(swap(lower, 1), ORDER_A, 1)
+    upper_y = reorder(swap(upper, 2), ORDER_B, 2)
+    lower_far = swap(jnp.concatenate([lower, lower_x], 1), 2)
+    upper_far = swap(jnp.concatenate([upper, upper_y], 1), 1)
+    lower_far = reorder(lower_far, ORDER_A, 2)
+    upper_far = reorder(upper_far, ORDER_B, 1)
+    width = own.shape[1]
+    return jnp.concatenate(
+        [
+            jnp.concatenate([lower, lower_x, lower_far], 1),
+            jnp.concatenate([upper, upper_far[:, :width], upper_y, upper_far[:, width:]], 1),
+        ],
+        0,
+    )
+
+
+def to_sequence(rows):
+    micro, tokens, width = rows.shape
+    quarter = tokens // 4
+    pieces = jnp.transpose(rows.reshape(micro, 4, quarter, width), (1, 0, 2, 3))
+    pieces = lax.all_to_all(pieces, "batch", 0, 0, tiled=True)
+    pieces = pieces.reshape(4 * micro, quarter, width)
+    pieces = lax.all_to_all(pieces, "seq", 0, 0, tiled=True)
+    return pieces.reshape(4 * micro * quarter, width)
+
+
+def from_sequence(rows, micro):
+    width = rows.shape[1]
+    quarter = rows.shape[0] // (4 * micro)
+    pieces = rows.reshape(4 * micro, quarter, width)
+    pieces = lax.all_to_all(pieces, "seq", 0, 0, tiled=True)
+    pieces = pieces.reshape(4, micro, quarter, width)
+    pieces = lax.all_to_all(pieces, "batch", 0, 0, tiled=True)
+    return jnp.transpose(pieces, (1, 0, 2, 3)).reshape(micro, 4 * quarter, width)
+
+
+def three_parts(value):
+    high = value.astype(jnp.bfloat16)
+    rest = value - high.astype(jnp.float32)
+    middle = rest.astype(jnp.bfloat16)
+    low = (rest - middle.astype(jnp.float32)).astype(jnp.bfloat16)
+    return high, middle, low
+
+
+def token_features(segments, variates):
+    lane = lax.broadcasted_iota(jnp.int32, (1, FEATURES), 1)
+    variate_hot = (lane < 12) & (lane % 4 == variates)
+    ones = (lane >= 12) & (lane < 15)
+    segment_lane = (lane >= 16) & (lane < LSE_AT)
+    segment_hot = segment_lane & (lane - 16 == segments)
+    query_side = variate_hot | ones | segment_hot
+    key_side = (
+        variate_hot
+        | ones
+        | (segment_lane & ~segment_hot)
+        | ((lane >= LSE_AT) & (lane < LSE_AT + 3))
+    )
+    return query_side.astype(jnp.bfloat16), key_side.astype(jnp.bfloat16)
+
+
+def head_weights(same_bias, other_bias):
+    gap = [part[:, None] for part in three_parts(same_bias - other_bias)]
+    base = [part[:, None] for part in three_parts(other_bias)]
+    heads = same_bias.shape[0]
+    columns = [jnp.broadcast_to(part, (heads, 4)) for part in gap] + base
+    columns.append(jnp.zeros((heads, 1), jnp.bfloat16))
+    columns.append(jnp.full((heads, LSE_AT - 16), MASKED, jnp.bfloat16))
+    columns.append(jnp.zeros((heads, FEATURES - LSE_AT), jnp.bfloat16))
+    return jnp.concatenate(columns, 1)
+
+
+def turn_pair(pair, cosine, sine):
+    lane = lax.broadcasted_iota(jnp.int32, pair.shape, 1)
+    crossed = jnp.where(lane % 64 < 32, pltpu.roll(pair, 96, 1), pltpu.roll(pair, 32, 1))
+    return pair * cosine + crossed * sine
+
+
+def dot_rows(left, right):
+    return lax.dot_general(left, right, (((1,), (1,)), ((), ())), preferred_element_type=jnp.float32)
+
+
+def dot_first(left, right):
+    return lax.dot_general(left, right, (((0,), (0,)), ((), ())), preferred_element_type=jnp.float32)
+
+
+def attend_kernel(
+    proj_ref,
+    cos_ref,
+    sin_ref,
+    query_side_ref,
+    key_side_ref,
+    weights_ref,
+    turned_ref,
+    wide_ref,
+    low_ref,
+    log_ref,
+    keys_ref,
+    values_ref,
+):
+    length = proj_ref.shape[0]
+    rows_at_once = 256
+    ones_lane = lax.broadcasted_iota(jnp.int32, (length, 128), 1) == 0
+    for pair in range(2):
+        at = 128 * pair
+        turned = turn_pair(
+            proj_ref[:, 256 + at : 384 + at], cos_ref[...], sin_ref[...]
+        ).astype(jnp.bfloat16)
+        turned_ref[:, 256 + at : 384 + at] = turned
+        keys_ref[pair, :, :128] = turned
+        keys_ref[pair, :, 128:] = key_side_ref[...]
+        value = proj_ref[:, 512 + at : 640 + at].astype(jnp.bfloat16)
+        turned_ref[:, 512 + at : 640 + at] = value
+        values_ref[pair, :, :128] = value
+        values_ref[pair, :, 128:] = ones_lane.astype(jnp.bfloat16)
+    half_lane = lax.broadcasted_iota(jnp.int32, (rows_at_once, 128), 1) // 64
+    lane = lax.broadcasted_iota(jnp.int32, (rows_at_once, 128), 1)
+
+    def one_block(index, carry):
+        rows = pl.ds(pl.multiple_of(index * rows_at_once, rows_at_once), rows_at_once)
+        cosine = cos_ref[rows, :]
+        sine = sin_ref[rows, :]
+        side = query_side_ref[rows, :]
+        logs = jnp.zeros((rows_at_once, 128), jnp.float32)
+        for pair in range(2):
+            at = 128 * pair
+            turned = turn_pair(proj_ref[rows, at : at + 128], cosine, sine).astype(jnp.bfloat16)
+            turned_ref[rows, at : at + 128] = turned
+            scaled = turned * jnp.bfloat16(SCORE_SCALE)
+            mixed = jnp.zeros((rows_at_once, 128), jnp.float32)
+            for half in range(2):
+                head = 2 * pair + half
+                query = jnp.concatenate(
+                    [
+                        jnp.where(half_lane == half, scaled, jnp.bfloat16(0)),
+                        side * weights_ref[head : head + 1, :],
+                    ],
+                    1,
+                )
+                scores = dot_rows(query, keys_ref[pair])
+                top = jnp.max(scores, 1, keepdims=True)
+                powers = jnp.exp(scores - top).astype(jnp.bfloat16)
+                summed = jnp.dot(powers, values_ref[pair], preferred_element_type=jnp.float32)
+                total = summed[:, 128:129]
+                mixed = jnp.where(half_lane == half, summed[:, :128] / total, mixed)
+                logs = jnp.where(lane == head, top + jnp.log(total), logs)
+            wide_ref[rows, at : at + 128] = mixed
+            low_ref[rows, at : at + 128] = mixed.astype(jnp.bfloat16)
+        log_ref[rows, :] = logs
+        return carry
+
+    lax.fori_loop(0, length // rows_at_once, one_block, 0)
+
+
+def attend_sequence(proj, cosine, sine, query_side, key_side, weights):
+    length = proj.shape[0]
+    return pl.pallas_call(
+        attend_kernel,
+        out_shape=(
+            jax.ShapeDtypeStruct((length, 768), jnp.bfloat16),
+            jax.ShapeDtypeStruct((length, 256), jnp.float32),
+            jax.ShapeDtypeStruct((length, 256), jnp.bfloat16),
+            jax.ShapeDtypeStruct((length, 128), jnp.float32),
+        ),
+        scratch_shapes=[
+            pltpu.VMEM((2, length, 256), jnp.bfloat16),
+            pltpu.VMEM((2, length, 256), jnp.bfloat16),
+        ],
+        cost_estimate=pl.CostEstimate(
+            flops=16 * length * length * 256, bytes_accessed=8 * 2**20, transcendentals=0
+        ),
+        name="attend",
+    )(proj, cosine, sine, query_side, key_side, weights)
+
+
+def attend_back_kernel(
+    turned_ref,
+    wide_ref,
+    log_ref,
+    grad_ref,
+    cos_ref,
+    sin_ref,
+    query_side_ref,
+    key_side_ref,
+    weights_ref,
+    out_ref,
+    bias_ref,
+    queries_ref,
+    grads_ref,
+    total_ref,
+):
+    length = turned_ref.shape[0]
+    rows_at_once = 256
+    half_lane = lax.broadcasted_iota(jnp.int32, (length, 128), 1) // 64
+    lane = lax.broadcasted_iota(jnp.int32, (length, 128), 1)
+    for pair in range(2):
+        at = 128 * pair
+        scaled = turned_ref[:, at : at + 128] * jnp.bfloat16(SCORE_SCALE)
+        grad = grad_ref[:, at : at + 128]
+        product = grad.astype(jnp.float32) * wide_ref[:, at : at + 128]
+        for half in range(2):
+            head = 2 * pair + half
+            side = query_side_ref[...] * weights_ref[head : head + 1, :]
+            for place, part in enumerate(three_parts(-log_ref[:, head : head + 1])):
+                side = jnp.where(lane == LSE_AT + place, part, side)
+            queries_ref[head, :, :128] = jnp.where(half_lane == half, scaled, jnp.bfloat16(0))
+            queries_ref[head, :, 128:] = side
+            delta = jnp.sum(jnp.where(half_lane == half, product, 0.0), 1, keepdims=True)
+            extra = jnp.zeros((length, 128), jnp.bfloat16)
+            for place, part in enumerate(three_parts(-delta)):
+                extra = jnp.where(lane == place, part, extra)
+            grads_ref[head, :, :128] = grad
+            grads_ref[head, :, 128:] = extra
+    total_ref[...] = jnp.zeros_like(total_ref)
+    half_short = half_lane[:rows_at_once]
+    lane_short = lane[:rows_at_once]
+    three_ones = (lane_short < 3).astype(jnp.bfloat16)
+
+    def one_block(index, carry):
+        rows = pl.ds(pl.multiple_of(index * rows_at_once, rows_at_once), rows_at_once)
+        cosine = cos_ref[rows, :]
+        sine = -sin_ref[rows, :]
+        key_side = key_side_ref[rows, :]
+        first_four = jnp.where(lane_short < 4, key_side.astype(jnp.float32), 0.0)
+        sums = list(carry)
+        for pair in range(2):
+            at = 128 * pair
+            keys = turned_ref[rows, 256 + at : 384 + at]
+            values = turned_ref[rows, 512 + at : 640 + at]
+            grad_keys = jnp.zeros((rows_at_once, 128), jnp.float32)
+            grad_values = jnp.zeros((rows_at_once, 128), jnp.float32)
+            for half in range(2):
+                head = 2 * pair + half
+                scores = dot_rows(jnp.concatenate([keys, key_side], 1), queries_ref[head])
+                weights = jnp.exp(scores)
+                grad_weights = dot_rows(
+                    jnp.concatenate(
+                        [jnp.where(half_short == half, values, jnp.bfloat16(0)), three_ones], 1
+                    ),
+                    grads_ref[head],
+                )
+                grad_values = jnp.where(
+                    half_short == half,
+                    jnp.dot(
+                        weights.astype(jnp.bfloat16),
+                        grads_ref[head, :, :128],
+                        preferred_element_type=jnp.float32,
+                    ),
+                    grad_values,
+                )
+                grad_scores = (weights * grad_weights).astype(jnp.bfloat16)
+                both = jnp.dot(
+                    grad_scores,
+                    jnp.concatenate([queries_ref[head, :, :128], query_side_ref[...]], 1),
+                    preferred_element_type=jnp.float32,
+                )
+                grad_keys = grad_keys + both[:, :128]
+                counted = both[:, 128:]
+                same = jnp.sum(counted * first_four, 0, keepdims=True)
+                every = jnp.sum(jnp.where(lane_short < 4, counted, 0.0), 0, keepdims=True)
+                sums[head] = sums[head] + same
+                sums[4 + head] = sums[4 + head] + (every - same)
+                total_ref[:, at : at + 128] += dot_first(
+                    grad_scores, jnp.where(half_short == half, keys, jnp.bfloat16(0))
+                )
+            out_ref[rows, 256 + at : 384 + at] = turn_pair(grad_keys, cosine, sine).astype(
+                jnp.bfloat16
+            )
+            out_ref[rows, 512 + at : 640 + at] = grad_values.astype(jnp.bfloat16)
+        return tuple(sums)
+
+    start = tuple(jnp.zeros((1, 128), jnp.float32) for _ in range(8))
+    sums = lax.fori_loop(0, length // rows_at_once, one_block, start)
+    for place in range(8):
+        bias_ref[place : place + 1, :] = sums[place]
+    for pair in range(2):
+        at = 128 * pair
+        out_ref[:, at : at + 128] = turn_pair(
+            total_ref[:, at : at + 128] * SCORE_SCALE, cos_ref[...], -sin_ref[...]
+        ).astype(jnp.bfloat16)
+
+
+def attend_sequence_back(turned, wide, logs, grads, cosine, sine, query_side, key_side, weights):
+    length = turned.shape[0]
+    return pl.pallas_call(
+        attend_back_kernel,
+        out_shape=(
+            jax.ShapeDtypeStruct((length, 768), jnp.bfloat16),
+            jax.ShapeDtypeStruct((8, 128), jnp.float32),
+        ),
+        scratch_shapes=[
+            pltpu.VMEM((4, length, 256), jnp.bfloat16),
+            pltpu.VMEM((4, length, 256), jnp.bfloat16),
+            pltpu.VMEM((length, 256), jnp.float32),
+        ],
+        cost_estimate=pl.CostEstimate(
+            flops=40 * length * length * 256, bytes_accessed=8 * 2**20, transcendentals=0
+        ),
+        name="attend_back",
+    )(turned, wide, logs, grads, cosine, sine, query_side, key_side, weights)
+
+
+def on_plane(
+    inputs,
+    w_query,
+    w_key,
+    w_value,
+    w_output,
+    gain_attention,
+    w_gate,
+    w_up,
+    w_down,
+    gain_feed,
+    variate_bias,
+    segment_ids,
+    variate_ids,
+    positions,
+    grad_output,
+):
+    low, wide = jnp.bfloat16, jnp.float32
+    rank = lax.axis_index("batch")
+    micro, tokens = inputs.shape[0], inputs.shape[2]
+    n_seq = lax.axis_size("seq")
+    shard = w_query.shape[0]
+    per = D // 4
+    ff = w_gate.shape[1]
+    ff_per = ff // 4
+    ff_piece = ff_per // n_seq
+    rows_in = inputs.reshape(micro, tokens, D)
+
+    def columns(weight):
+        return lax.dynamic_slice_in_dim(weight, rank * per, per, 1)
+
+    gain_columns = jnp.concatenate(
+        [gain_attention[:, None], gain_feed[:, None], jnp.zeros((shard, 126), low)], 1
+    )
+    first_shard = jnp.concatenate(
+        [columns(w_query), columns(w_key), columns(w_value), w_output, gain_columns], 1
+    )
+
+    def ff_columns(weight):
+        cut = weight.reshape(shard, n_seq, 4 * ff_piece)
+        return lax.dynamic_slice_in_dim(cut, rank * ff_piece, ff_piece, 2).reshape(shard, ff_per)
+
+    down_rows = lax.dynamic_slice_in_dim(w_down, rank * ff_piece, ff_piece, 0)
+    first_weights = lax.all_gather(first_shard, "seq", axis=0, tiled=True)
+    second_shard = jnp.concatenate([ff_columns(w_gate), ff_columns(w_up)], 1)
+    second_weights = lax.all_gather(second_shard, "seq", axis=0, tiled=True)
+    down_weights = lax.all_gather(down_rows, "seq", axis=0, tiled=True)
+    gains = jnp.transpose(first_weights[:, 3 * per + D : 3 * per + D + 2]).astype(wide)
+    gain_first, gain_second = gains[0:1], gains[1:2]
+    qkv_weights = first_weights[:, : 3 * per]
+    out_weights = by_rank(
+        first_weights[:, 3 * per : 3 * per + D].reshape(4, per, D), rank
+    ).reshape(D, D)
+
+    numbers = jnp.stack(
+        [segment_ids, variate_ids, positions // 32, positions % 32], -1
+    ).reshape(micro, tokens, 4)
+    numbers = jnp.pad(numbers.astype(low), ((0, 0), (0, 0), (0, 124)))
+    mine = to_sequence(jnp.concatenate([rows_in, numbers], 2))
+    cot_mine = to_sequence(grad_output.reshape(micro, tokens, D))
+    whole = jnp.concatenate(gather_plane(mine), 0)
+    cot_low = jnp.concatenate(gather_plane(cot_mine), 0)
+    length = whole.shape[0]
+    quarter = length // 4
+    eighth = quarter // 2
+
+    def own(rows):
+        return jnp.concatenate([rows[:eighth], rows[2 * quarter : 2 * quarter + eighth]], 0)
+
+    numbers = whole[:, D : D + 4].astype(jnp.int32)
+    segments, variates = numbers[:, 0:1], numbers[:, 1:2]
+    places = (numbers[:, 2:3] * 32 + numbers[:, 3:4]).astype(wide)
+    lane = jnp.arange(128)
+    freqs = jnp.exp((lane % 32).astype(wide) * (-2.0 * math.log(10000.0) / HD))
+    angles = places * freqs[None, :]
+    cosine = jnp.cos(angles)
+    sine = jnp.where((lane % 64 < 32)[None, :], -jnp.sin(angles), jnp.sin(angles))
+    query_side, key_side = token_features(segments, variates)
+    my_bias = lax.dynamic_slice_in_dim(variate_bias, rank * 4, 4, 1)
+    weights = jnp.pad(head_weights(my_bias[0], my_bias[1]), ((0, 4), (0, 0)))
+
+    residual = whole[:, :D].astype(wide)
+    scale_first = lax.rsqrt(jnp.mean(residual * residual, -1, keepdims=True) + EPSILON)
+    mixed_first = (residual * scale_first * gain_first).astype(low)
+    proj = jnp.dot(mixed_first, qkv_weights, preferred_element_type=wide)
+    turned, attended_wide, attended_low, logs = attend_sequence(
+        proj, cosine, sine, query_side, key_side, weights
+    )
+    attended = gather_heads(attended_low)
+    middle = residual + jnp.dot(attended, out_weights, preferred_element_type=wide)
+    scale_second = lax.rsqrt(jnp.mean(middle * middle, -1, keepdims=True) + EPSILON)
+    mixed_second = (middle * scale_second * gain_second).astype(low)
+    gate_up = jnp.dot(mixed_second, second_weights, preferred_element_type=wide)
+    gate_proj, up_proj = gate_up[:, :ff_per], gate_up[:, ff_per:]
+    sigmoid_gate = jax.nn.sigmoid(gate_proj)
+    silu_gate = gate_proj * sigmoid_gate
+    hidden = (silu_gate * up_proj).astype(low)
+
+    grad_hidden = dot_rows(cot_low, down_weights)
+    silu_slope = sigmoid_gate * (1.0 + gate_proj * (1.0 - sigmoid_gate))
+    grad_gate_up = jnp.concatenate(
+        [(grad_hidden * up_proj * silu_slope).astype(low), (grad_hidden * silu_gate).astype(low)],
+        1,
+    )
+    grad_mixed_part = dot_rows(grad_gate_up, second_weights).astype(low)
+    grad_mixed_second = scatter_plane(grad_mixed_part).astype(wide)
+    out_part = jnp.dot(hidden, down_weights, preferred_element_type=wide).astype(low)
+    block_rows = (own(middle) + scatter_plane(out_part).astype(wide)).astype(low)
+    block_output = from_sequence(block_rows, micro).reshape(inputs.shape)
+    grad_down = dot_first(hidden, cot_low).astype(low)
+    grad_gate_up_weights = dot_first(mixed_second, grad_gate_up).astype(low)
+    shard_down = lax.psum_scatter(grad_down, "seq", scatter_dimension=0, tiled=True)
+    shard_gate_up = lax.psum_scatter(grad_gate_up_weights, "seq", scatter_dimension=0, tiled=True)
+
+    own_scale_second = own(scale_second)
+    grad_middle = cot_mine.astype(wide) + norm_back(
+        grad_mixed_second * gain_second, own(middle) * own_scale_second, own_scale_second
+    )
+    grad_branch = grad_middle.astype(low)
+    grad_attended = dot_rows(grad_branch, out_weights).astype(low)
+    branch_columns = by_rank(
+        jnp.transpose(grad_branch.reshape(quarter, 4, per), (1, 0, 2)), rank
+    )
+    parcels = [
+        jnp.concatenate([grad_attended[:, r * per : (r + 1) * per], branch_columns[r]], 1)
+        for r in range(4)
+    ]
+    parcels = [parcels[0]] + [swap(parcels[r], r) for r in range(1, 4)]
+    arrived = jnp.concatenate(
+        [parcels[r][:eighth] for r in ORDER_A] + [parcels[r][eighth:] for r in ORDER_B], 0
+    )
+    grad_heads, branch_mine = arrived[:, :per], arrived[:, per:]
+    grad_proj, bias_sums = attend_sequence_back(
+        turned,
+        attended_wide,
+        logs,
+        grad_heads,
+        cosine,
+        sine,
+        query_side,
+        key_side,
+        weights,
+    )
+    grad_first_part = dot_rows(grad_proj, qkv_weights).astype(low)
+    grad_mixed_first = scatter_plane(grad_first_part).astype(wide)
+    own_scale_first = own(scale_first)
+    grad_rows = grad_middle + norm_back(
+        grad_mixed_first * gain_first,
+        mine[:, :D].astype(wide) * own_scale_first,
+        own_scale_first,
+    )
+    grad_inputs = from_sequence(grad_rows.astype(low), micro).astype(wide).reshape(inputs.shape)
+
+    grad_out = dot_first(attended, branch_mine)
+    grad_out = by_rank(grad_out.reshape(4, per, per), rank).reshape(D, per)
+    grad_first_weights = jnp.concatenate([dot_first(mixed_first, grad_proj), grad_out], 1)
+    shard_first = lax.psum_scatter(
+        grad_first_weights.astype(low), "seq", scatter_dimension=0, tiled=True
+    )
+
+    def all_ranks(rows):
+        lower, lower_far, upper, upper_far = gather_plane(rows)
+        half = rows.shape[0] // 2
+        blocks = [
+            (lower[:half], upper[:half]),
+            (lower[half:], upper_far[:half]),
+            (lower_far[:half], upper[half:]),
+            (lower_far[half:], upper_far[half:]),
+        ]
+        return by_rank(jnp.stack([jnp.concatenate(pair, 0) for pair in blocks]), rank)
+
+    full_gate_up = all_ranks(shard_gate_up).astype(wide)
+    full_down = all_ranks(shard_down).astype(wide)
+
+    def ff_whole(blocks):
+        cut = blocks.reshape(4, shard, n_seq, ff_piece)
+        return jnp.transpose(cut, (1, 2, 0, 3)).reshape(shard, ff)
+
+    grad_gate = ff_whole(full_gate_up[:, :, :ff_per])
+    grad_up = ff_whole(full_gate_up[:, :, ff_per:])
+    grad_down = full_down.reshape(4 * ff_piece, D)
+    full_first = all_ranks(shard_first).astype(wide)
+    grad_query, grad_key, grad_value, grad_output_weights = [
+        jnp.transpose(full_first[:, :, i * per : (i + 1) * per], (1, 0, 2)).reshape(shard, D)
+        for i in range(4)
+    ]
+
+    def gain_grad(pairs, gain):
+        total = sum(jnp.sum(weight.astype(wide) * grad, 1) for weight, grad in pairs)
+        return total / gain.astype(wide)
+
+    grad_gain_first = gain_grad(
+        [(w_query, grad_query), (w_key, grad_key), (w_value, grad_value)], gain_attention
+    )
+    grad_gain_second = gain_grad([(w_gate, grad_gate), (w_up, grad_up)], gain_feed)
+    bias_part = jnp.sum(bias_sums, 1).reshape(2, 4)
+    bias_part = lax.dynamic_update_slice(jnp.zeros((2, H), wide), bias_part, (0, rank * 4))
+    grad_bias = lax.psum(bias_part, ("batch", "seq"))
+    return (
+        block_output,
+        grad_inputs,
+        grad_query,
+        grad_key,
+        grad_value,
+        grad_output_weights,
+        grad_gain_first,
+        grad_gate,
+        grad_up,
+        grad_down,
+        grad_gain_second,
+        grad_bias,
+    )
+
+
 def solution(mesh):
+    n_batch, n_seq = mesh.shape["batch"], mesh.shape["seq"]
+    step = on_plane if n_batch == 4 and n_seq == 8 else on_device
     return jax.shard_map(
-        on_device,
+        step,
         mesh=mesh,
         in_specs=(
             P(None, "batch", "seq", None),

time: 2150 us -> 604 us (0.28)
  waiting for transfers between devices: 841 us -> 181 us
  starting transfers between devices: 702 us -> 93.3 us
  matrix products: 238 us -> 66.4 us
  other arithmetic: 129 us -> 67.8 us
  blocking collectives: 103 us -> 52.3 us
  between operations: 51.8 us -> 15.8 us
  Pallas kernels: 0 us -> 31.1 us
    ppermute x192 -> x39, starting transfers between devices: 702 us -> 50.6 us  [swap(): return lax.ppermute(value, 'batch', [(i, i ^ bit) for i in range(4)])]
    reduce_scatter x7 -> x2, waiting for transfers between devices: 643 us -> 0.03 us  [the longest x1 0.02 us: on_plane(): lax.psum_scatter(grad_gate_up_weights, 'seq', scatter_dimension=0, tiled=...]
    dot_general x101 -> x12, matrix products: 238 us -> 66.4 us  [the longest x4 23.1 us: dot_rows(): lax.dot_general(left, right, (((1,), (1,)), ((), ())), preferred_element_...]
    all_to_all x0 -> x7, waiting for transfers between devices: none -> 66.9 us  [the longest x2 42 us: to_sequence(): pieces = lax.all_to_all(pieces, 'seq', 0, 0, tiled=True)]
    convert_element_type x73 -> x15, other arithmetic: 77.6 us -> 14.1 us  [the longest x2 6.12 us: on_plane(): grad_branch = grad_middle.astype(low)]
    all_gather x7 -> x3, waiting for transfers between devices: 62.4 us -> 0.01 us  [the longest x1 0.01 us: on_plane(): second_weights = lax.all_gather(second_shard, 'seq', axis=0, tiled=True)]
    all_to_all x0 -> x7, starting transfers between devices: none -> 42.3 us  [the longest x2 21 us: from_sequence(): pieces = lax.all_to_all(pieces, 'seq', 0, 0, tiled=True)]
    all_gather x2 -> x0, blocking collectives: 39.8 us -> none  [the longest x1 26.3 us: on_device(): lax.all_gather(gain_feed, 'seq', axis=0, tiled=True)]
  transfers between devices with their start and end apart: 207 -> 52, of which waited for: 32 -> 31; matrix products, arithmetic and copies ran while one was open for 17% -> 29% of each run, Pallas kernels for 0% -> 5%
where the time goes in v1:
time: 604 us; the launch traced here: 594 us
  waiting for transfers between devices  181 us (30%)
  starting transfers between devices  93.3 us (15%)
  local copies, waits for them, and re-layouts  86.1 us (14%)
  other arithmetic  67.8 us (11%)
  matrix products  66.4 us (11%)
  blocking collectives  52.3 us (9%)
  Pallas kernels  31.1 us (5%)
  between operations  15.8 us (3%)
    ppermute x39, waiting for transfers between devices, swap(): return lax.ppermute(value, 'batch', [(i, i ^ bit) for i in range(4)])  114 us
    ppermute x39, starting transfers between devices, swap(): return lax.ppermute(value, 'batch', [(i, i ^ bit) for i in range(4)])  50.6 us
    all_to_all x2, waiting for transfers between devices, to_sequence(): pieces = lax.all_to_all(pieces, 'seq', 0, 0, tiled=True)  42 us
    psum x1, blocking collectives, on_plane(): grad_bias = lax.psum(bias_part, ('batch', 'seq'))  40.2 us
    unnamed x141, local copies, waits for them, and re-layouts  27 us
    dot_general x4, matrix products, dot_rows(): lax.dot_general(left, right, (((1,), (1,)), ((), ())), preferred_element_...  23.1 us
    concatenate x1, other arithmetic, gather_heads(): jnp.concatenate([jnp.concatenate([lower, lower_x, lower_far], 1), jnp.con...  21.4 us
    all_to_all x2, starting transfers between devices, from_sequence(): pieces = lax.all_to_all(pieces, 'seq', 0, 0, tiled=True)  21 us
  transfers between devices with their start and end apart: 52, of which 31 were waited for; matrix products, arithmetic and copies ran while one was open for 29% of the time, Pallas kernels for 5%

profile of v1, /device:TPU:0, one launch (start us, length us, event | category | flops | bytes accessed | tf_op | source)
XLA Modules:
  0.0 594.1 jit_solution(11594397967448306549)
XLA Ops:
  17.4 5.2 all-to-all-start.4
  22.9 8.2 %all-to-all-done.4 = bf16[4,2,32,1024]{3,2,1,0:T(8,128)(2,1)} async-done(((bf16[4,2,32,1024]{3,2,1,0:T(8,128)(2,1)}), bf16[4,2,32,1024]{3,2,1,0:T(8,128)(2,1)}, u32[]{:S(2)}, u32[]{:S(2)}) %all-to-all-start.4) | async-done | bytes 524320 | tf_op jit(solution)/shard_map/all_to_all | solution.py:531
  31.1 12.1 %all_to_all.40 = bf16[4,2,32,1152]{3,2,1,0:T(8,128)(2,1)} all-to-all(bf16[4,2,32,1152]{3,2,1,0:T(8,128)(2,1)S(1)} %copy_bitcast_fusion), channel_id=1, replica_groups=mesh['batch'=4,'seq'=8] {'batch'}, dimensions={0} | all-to-all | bytes 1179648 | tf_op jit(solution)/shard_map/all_to_all | solution.py:531
  43.2 4.9 all-to-all-start.5
  49.3 20.6 %all-to-all-done.5 = bf16[8,32,1024]{2,1,0:T(8,128)(2,1)S(1)} async-done(((bf16[8,32,1024]{2,1,0:T(8,128)(2,1)}), bf16[8,32,1024]{2,1,0:T(8,128)(2,1)S(1)}, u32[]{:S(2)}, u32[]{:S(2)}) %all-to-all-start.5) | async-done | bytes 524320 | tf_op jit(solution)/shard_map/all_to_all | solution.py:533
  79.9 21.4 %all-to-all-done.1 = bf16[8,32,1152]{2,1,0:T(8,128)(2,1)S(1)} async-done(((bf16[8,32,1152]{2,1,0:T(8,128)(2,1)}), bf16[8,32,1152]{2,1,0:T(8,128)(2,1)S(1)}, u32[]{:S(2)}, u32[]{:S(2)}) %all-to-all-start.1) | async-done | bytes 589856 | tf_op jit(solution)/shard_map/all_to_all | solution.py:533
  114.4 10.1 %collective-permute-done.13 = bf16[256,1024]{1,0:T(8,128)(2,1)S(1)} collective-permute-done((bf16[256,1024]{1,0:T(8,128)(2,1)S(1)}, bf16[256,1024]{1,0:T(8,128)(2,1)S(1)}, u32[]{:S(2)}, u32[]{:S(2)}) %collective-permute-start.13) | collective-permute-done | bytes 524320 | tf_op jit(solution)/shard_map/ppermute | solution.py:478
  126.8 6.3 %collective-permute-done.1 = bf16[256,1152]{0,1:T(8,128)(2,1)S(1)} collective-permute-done((bf16[256,1152]{0,1:T(8,128)(2,1)S(1)}, bf16[256,1152]{0,1:T(8,128)(2,1)S(1)}, u32[]{:S(2)}, u32[]{:S(2)}) %collective-permute-start.1) | collective-permute-done | bytes 589856 | tf_op jit(solution)/shard_map/ppermute | solution.py:478
  140.7 5.8 fusion.15.proj_ref
  146.5 12.0 %attend.1 = (bf16[1024,768]{1,0:T(8,128)(2,1)}, f32[1024,256]{1,0:T(8,128)}, bf16[1024,256]{1,0:T(8,128)(2,1)}, f32[1024,128]{1,0:T(8,128)}) custom-call(f32[1024,768]{1,0:T(8,128)} %fusion.15.proj_ref, f32[1024,128]{1,0:T(8,128)} %get-tuple-element.185.cos_ref, f32[1024,128]{1,0:T(8,128)} %get-tuple-element.184.sin_ref, ...), custom_call_target="tpu_custom_call" | custom-call | flops 4294967296 | bytes 8388608 | tf_op jit(solution)/shard_map/attend/pallas_call | solution.py:666
  166.9 5.3 collective-permute-done.4
  173.2 5.4 collective-permute-done.7
  181.6 21.4 %fusion.12 = bf16[1024,1024]{1,0:T(8,128)(2,1)S(1)} fusion(bf16[256,512]{1,0:T(8,128)(2,1)S(1)} %get-tuple-element.152, bf16[256,512]{1,0:T(8,128)(2,1)S(1)} %get-tuple-element.151, bf16[128,256]{1,0:T(8,128)(2,1)S(1)} %get-tuple-element.174, bf16[128,256]{1,0:T(8,128)(2,1)S(1)} %get-tuple-element.175, bf16[128,256]{1,0:T(8,128)(2,1)S(1)} %get-tuple-element.176, ...), kind=kLoop, calls=%fused_computation.25 | loop fusion | flops 38797312 | bytes 4456448 | tf_op jit(solution)/shard_map/concatenate | solution.py:518
  203.0 4.8 multiply_reduce_fusion
  207.9 11.5 %fusion.47 = f32[1024,2048]{1,0:T(8,128)} fusion(bf16[1024,2048]{1,0:T(8,128)(2,1)} %all-gather.6.cloned.1.call-done, f32[1024,1024]{0,1:T(8,128)} %get-tuple-element.199, f32[1024]{0:T(1024)S(1)} %get-tuple-element.84, f32[1024]{0:T(1024)S(1)} %add_rsqrt_fusion), kind=kOutput, calls=%fused_computation.243 | convolution fusion | flops 4298113024 | bytes 16785408 | tf_op jit(solution)/shard_map/dot_general | solution.py:904
  219.4 10.5 %multiply_convert_fusion.1 = (bf16[1024,1024]{1,0:T(8,128)(2,1)}, bf16[1024,1024]{1,0:T(8,128)(2,1)}, bf16[1024,1024]{1,0:T(8,128)(2,1)S(1)}) fusion(f32[1024,2048]{1,0:T(8,128)} %fusion.47, bf16[1024,1024]{1,0:T(8,128)(2,1)} %constant_dynamic-update-slice_fusion.6, bf16[1024,1024]{1,0:T(8,128)(2,1)} %all-gather.8.cloned.1.call-done), kind=kOutput, calls=%fused_computation.13 | convolution fusion | flops 2163212288 | bytes 18874368 | tf_op jit(solution)/shard_map/dot_general | solution.py:589
  235.4 8.1 %fusion.13 = bf16[1024,1024]{0,1:T(8,128)(2,1)S(1)} fusion(bf16[1024,2048]{1,0:T(8,128)(2,1)} %all-gather.6.cloned.1.call-done, bf16[1024,1024]{1,0:T(8,128)(2,1)} %get-tuple-element.89, bf16[1024,1024]{1,0:T(8,128)(2,1)} %get-tuple-element.88), kind=kOutput, calls=%fused_computation.34 | convolution fusion | flops 4304404480 | bytes 10485760 | tf_op jit(solution)/shard_map/dot_general | solution.py:589
  249.5 6.0 %collective-permute-done.16 = bf16[256,1024]{0,1:T(8,128)(2,1)S(1)} collective-permute-done((bf16[256,1024]{0,1:T(8,128)(2,1)S(1)}, bf16[256,1024]{0,1:T(8,128)(2,1)S(1)}, u32[]{:S(2)}, u32[]{:S(2)}) %collective-permute-start.16) | collective-permute-done | bytes 524320 | tf_op jit(solution)/shard_map/ppermute | solution.py:478
  269.1 9.1 %collective-permute-done.9 = bf16[128,1024]{1,0:T(8,128)(2,1)} collective-permute-done((bf16[128,1024]{1,0:T(8,128)(2,1)}, bf16[128,1024]{1,0:T(8,128)(2,1)}, u32[]{:S(2)}, u32[]{:S(2)}) %collective-permute-start.9) | collective-permute-done | bytes 262176 | tf_op jit(solution)/shard_map/ppermute | solution.py:478
  313.2 5.7 collective-permute-done.21
  326.8 19.0 %attend_back.1 = (bf16[1024,768]{1,0:T(8,128)(2,1)}, f32[8,128]{1,0:T(8,128)}) custom-call(bf16[1024,768]{1,0:T(8,128)(2,1)} %get-tuple-element.19.turned_ref, f32[1024,256]{1,0:T(8,128)} %get-tuple-element.20.wide_ref, f32[1024,128]{1,0:T(8,128)} %get-tuple-element.21.log_ref, bf16[1024,256]{1,0:T(8,128)(2,1)} %slice.538.grad_ref, ...), custom_call_target="tpu_custom_call" | custom-call | flops 10737418240 | bytes 8388608 | tf_op jit(solution)/shard_map/attend_back/pallas_call | solution.py:794
  355.4 10.1 %convolution_convert_fusion = bf16[1024,2048]{1,0:T(8,128)(2,1)} fusion(bf16[1024,1024]{1,0:T(8,128)(2,1)} %get-tuple-element.89, bf16[1024,1024]{1,0:T(8,128)(2,1)} %get-tuple-element.88, f32[1024,1024]{0,1:T(8,128)} %get-tuple-element.199, f32[1024]{0:T(1024)S(1)} %get-tuple-element.84, f32[1024]{0:T(1024)S(1)} %add_rsqrt_fusion), kind=kOutput, calls=%fused_computation.19 | convolution fusion | flops 4308598784 | bytes 12591104 | tf_op jit(solution)/shard_map/dot_general | solution.py:593
  371.5 14.1 %all-to-all-start.2 = ((bf16[8,32,1024]{2,1,0:T(8,128)(2,1)}), bf16[8,32,1024]{2,1,0:T(8,128)(2,1)}, u32[]{:S(2)}, u32[]{:S(2)}) async-start(bf16[8,32,1024]{2,1,0:T(8,128)(2,1)} %get-tuple-element.122), calls=%async_computation.2 | async-start | bytes 1048576 | tf_op jit(solution)/shard_map/all_to_all | solution.py:541
  396.3 6.5 %collective-permute-done.25 = bf16[256,1024]{0,1:T(8,128)(2,1)} collective-permute-done((bf16[256,1024]{0,1:T(8,128)(2,1)}, bf16[256,1024]{0,1:T(8,128)(2,1)}, u32[]{:S(2)}, u32[]{:S(2)}) %collective-permute-start.25) | collective-permute-done | bytes 524320 | tf_op jit(solution)/shard_map/ppermute | solution.py:478
  420.2 6.9 %all-to-all-start.6 = ((bf16[8,32,1024]{2,1,0:T(8,128)(2,1)}), bf16[8,32,1024]{2,1,0:T(8,128)(2,1)}, u32[]{:S(2)}, u32[]{:S(2)}) async-start(bf16[8,32,1024]{2,1,0:T(8,128)(2,1)} %bitcast.47), calls=%async_computation.6 | async-start | bytes 1048576 | tf_op jit(solution)/shard_map/all_to_all | solution.py:541
  429.3 4.8 collective-permute-done.36
  434.7 16.6 %all-to-all-done.6 = bf16[8,32,1024]{2,1,0:T(8,128)(2,1)} async-done(((bf16[8,32,1024]{2,1,0:T(8,128)(2,1)}), bf16[8,32,1024]{2,1,0:T(8,128)(2,1)}, u32[]{:S(2)}, u32[]{:S(2)}) %all-to-all-start.6) | async-done | bytes 524320 | tf_op jit(solution)/shard_map/all_to_all | solution.py:541
  455.1 40.2 %psum.7 = f32[2,16]{1,0:T(2,128)} all-reduce(f32[2,16]{1,0:T(2,128)S(1)} %dynamic_update_slice.3), channel_id=1, replica_groups=mesh['batch'=4,'seq'=8] {'batch','seq'}, use_global_device_ids=true, to_apply=%region_13.14 | all-reduce | flops 32 | bytes 256 | tf_op jit(solution)/shard_map/psum | solution.py:1009
  530.4 5.5 collective-permute-done.30
  539.2 4.4 collective-permute-done.32
  547.2 6.6 %collective-permute-done.33 = bf16[128,2048]{1,0:T(8,128)(2,1)S(1)} collective-permute-done((bf16[128,2048]{1,0:T(8,128)(2,1)}, bf16[128,2048]{1,0:T(8,128)(2,1)S(1)}, u32[]{:S(2)}, u32[]{:S(2)}) %collective-permute-start.33) | collective-permute-done | bytes 524320 | tf_op jit(solution)/shard_map/ppermute | solution.py:478
  561.5 5.5 collective-permute-done.34
  (418 shorter events, 243.5 us)
Async XLA Ops:
  7.2 132.0 %all-gather.4.cloned.1.call-start = ((), (), s32[]{:S(2)}) async-start(), calls=%async_computation.11 | async-start | bytes 4423680 | tf_op jit(solution)/shard_map/all_gather | solution.py:855
  12.6 195.3 %all-gather.6.cloned.1.call-start = ((), (), s32[]{:S(2)}) async-start(), calls=%async_computation.12 | async-start | bytes 4718592 | tf_op jit(solution)/shard_map/all_gather | solution.py:857
  17.4 13.7 %all-to-all-start.4 = ((bf16[4,2,32,1024]{3,2,1,0:T(8,128)(2,1)}), bf16[4,2,32,1024]{3,2,1,0:T(8,128)(2,1)}, u32[]{:S(2)}, u32[]{:S(2)}) async-start(bf16[4,2,32,1024]{3,2,1,0:T(8,128)(2,1)} %bitcast.172), calls=%async_computation.4 | async-start | bytes 1048576 | tf_op jit(solution)/shard_map/all_to_all | solution.py:531
  43.2 26.7 %all-to-all-start.5 = ((bf16[8,32,1024]{2,1,0:T(8,128)(2,1)}), bf16[8,32,1024]{2,1,0:T(8,128)(2,1)S(1)}, u32[]{:S(2)}, u32[]{:S(2)}) async-start(bf16[8,32,1024]{2,1,0:T(8,128)(2,1)} %bitcast.30), calls=%async_computation.5 | async-start | bytes 1048576 | tf_op jit(solution)/shard_map/all_to_all | solution.py:533
  48.1 171.2 %all-gather.8.cloned.1.call-start = ((), (), s32[]{:S(2)}) async-start(), calls=%async_computation.13 | async-start | bytes 2359296 | tf_op jit(solution)/shard_map/all_gather | solution.py:858
  69.9 31.4 %all-to-all-start.1 = ((bf16[8,32,1152]{2,1,0:T(8,128)(2,1)}), bf16[8,32,1152]{2,1,0:T(8,128)(2,1)S(1)}, u32[]{:S(2)}, u32[]{:S(2)}) async-start(bf16[8,32,1152]{2,1,0:T(8,128)(2,1)} %bitcast.10), calls=%async_computation.1 | async-start | bytes 1179648 | tf_op jit(solution)/shard_map/all_to_all | solution.py:533
  73.4 353.7 %reduce-scatter.8.cloned.1.call-start = ((), (), s32[]{:S(2)}) async-start(), calls=%async_computation.15 | async-start | bytes 2359296 | tf_op jit(solution)/shard_map/reduce_scatter | solution.py:923
  74.7 30.2 %collective-permute-start.12 = (bf16[128,1024]{1,0:T(8,128)(2,1)S(1)}, bf16[128,1024]{1,0:T(8,128)(2,1)}, u32[]{:S(2)}, u32[]{:S(2)}) collective-permute-start(bf16[128,1024]{1,0:T(8,128)(2,1)S(1)} %bitcast.200), channel_id=1, source_target_pairs={{0,8},{8,0},{16,24},{24,16},{1,9},{9,1},{17,25},{25,17},{2,10},{10... | collective-permute-start | bytes 786440 | tf_op jit(solution)/shard_map/ppermute | solution.py:478
  76.2 30.3 %collective-permute-start.14 = (bf16[128,1024]{1,0:T(8,128)(2,1)S(1)}, bf16[128,1024]{1,0:T(8,128)(2,1)S(1)}, u32[]{:S(2)}, u32[]{:S(2)}) collective-permute-start(bf16[128,1024]{1,0:T(8,128)(2,1)S(1)} %bitcast.197), channel_id=1, source_target_pairs={{0,16},{8,24},{16,0},{24,8},{1,17},{9,25},{17,1},{25,9},{2,18},{10... | collective-permute-start | bytes 786440 | tf_op jit(solution)/shard_map/ppermute | solution.py:478
  105.9 18.6 %collective-permute-start.13 = (bf16[256,1024]{1,0:T(8,128)(2,1)S(1)}, bf16[256,1024]{1,0:T(8,128)(2,1)S(1)}, u32[]{:S(2)}, u32[]{:S(2)}) collective-permute-start(bf16[256,1024]{1,0:T(8,128)(2,1)S(1)} %pad_maximum_fusion.19), channel_id=1, source_target_pairs={{0,16},{8,24},{16,0},{24,8},{1,17},{9,25},{17,1},{25,9},{2,18},{10... | collective-permute-start | bytes 1572872 | tf_op jit(solution)/shard_map/ppermute | solution.py:478
  107.3 53.8 %collective-permute-start.15 = (bf16[256,1024]{1,0:T(8,128)(2,1)}, bf16[256,1024]{1,0:T(8,128)(2,1)}, u32[]{:S(2)}, u32[]{:S(2)}) collective-permute-start(bf16[256,1024]{1,0:T(8,128)(2,1)} %pad_maximum_fusion.20), channel_id=1, source_target_pairs={{0,8},{8,0},{16,24},{24,16},{1,9},{9,1},{17,25},{25,17},{2,10},{10... | collective-permute-start | bytes 1572872 | tf_op jit(solution)/shard_map/ppermute | solution.py:478
  110.1 23.0 %collective-permute-start.1 = (bf16[256,1152]{0,1:T(8,128)(2,1)S(1)}, bf16[256,1152]{0,1:T(8,128)(2,1)S(1)}, u32[]{:S(2)}, u32[]{:S(2)}) collective-permute-start(bf16[256,1152]{0,1:T(8,128)(2,1)S(1)} %pad_maximum_fusion.15), channel_id=1, source_target_pairs={{0,16},{8,24},{16,0},{24,8},{1,17},{9,25},{17,1},{25,9},{2,18},{10... | collective-permute-start | bytes 1769480 | tf_op jit(solution)/shard_map/ppermute | solution.py:478
  113.4 20.0 %collective-permute-start.3 = (bf16[256,1152]{0,1:T(8,128)(2,1)S(1)}, bf16[256,1152]{0,1:T(8,128)(2,1)S(1)}, u32[]{:S(2)}, u32[]{:S(2)}) collective-permute-start(bf16[256,1152]{0,1:T(8,128)(2,1)S(1)} %pad_maximum_fusion.16), channel_id=1, source_target_pairs={{0,8},{8,0},{16,24},{24,16},{1,9},{9,1},{17,25},{25,17},{2,10},{10... | collective-permute-start | bytes 1769480 | tf_op jit(solution)/shard_map/ppermute | solution.py:478
  166.1 12.5 %collective-permute-start.7 = (bf16[512,512]{1,0:T(8,128)(2,1)S(1)}, bf16[512,512]{1,0:T(8,128)(2,1)S(1)}, u32[]{:S(2)}, u32[]{:S(2)}) collective-permute-start(bf16[512,512]{1,0:T(8,128)(2,1)S(1)} %maximum_maximum_fusion.1), channel_id=1, source_target_pairs={{0,8},{8,0},{16,24},{24,16},{1,9},{9,1},{17,25},{25,17},{2,10},{10... | collective-permute-start | bytes 1572872 | tf_op jit(solution)/shard_map/ppermute | solution.py:478
  235.3 273.9 %reduce-scatter.10.cloned.1.call-start = ((), (), s32[]{:S(2)}) async-start(), calls=%async_computation.16 | async-start | bytes 2359296
  243.6 11.9 %collective-permute-start.16 = (bf16[256,1024]{0,1:T(8,128)(2,1)S(1)}, bf16[256,1024]{0,1:T(8,128)(2,1)S(1)}, u32[]{:S(2)}, u32[]{:S(2)}) collective-permute-start(bf16[256,1024]{0,1:T(8,128)(2,1)S(1)} %slice.519), channel_id=1, source_target_pairs={{0,16},{8,24},{16,0},{24,8},{1,17},{9,25},{17,1},{25,9},{2,18},{10... | collective-permute-start | bytes 1572872 | tf_op jit(solution)/shard_map/ppermute | solution.py:478
  246.6 14.5 %collective-permute-start.8 = (bf16[256,1024]{1,0:T(8,128)(2,1)S(1)}, bf16[256,1024]{1,0:T(8,128)(2,1)S(1)}, u32[]{:S(2)}, u32[]{:S(2)}) collective-permute-start(bf16[256,1024]{1,0:T(8,128)(2,1)S(1)} %slice.509), channel_id=1, source_target_pairs={{0,16},{8,24},{16,0},{24,8},{1,17},{9,25},{17,1},{25,9},{2,18},{10... | collective-permute-start | bytes 1572872 | tf_op jit(solution)/shard_map/ppermute | solution.py:478
  257.2 11.0 %collective-permute-start.17 = (bf16[128,1024]{0,1:T(8,128)(2,1)}, bf16[128,1024]{0,1:T(8,128)(2,1)S(1)}, u32[]{:S(2)}, u32[]{:S(2)}) collective-permute-start(bf16[128,1024]{0,1:T(8,128)(2,1)} %slice.521), channel_id=1, source_target_pairs={{0,8},{8,0},{16,24},{24,16},{1,9},{9,1},{17,25},{25,17},{2,10},{10... | collective-permute-start | bytes 786440 | tf_op jit(solution)/shard_map/ppermute | solution.py:478
  258.9 20.3 %collective-permute-start.18 = (bf16[256,1024]{0,1:T(8,128)(2,1)}, bf16[256,1024]{0,1:T(8,128)(2,1)}, u32[]{:S(2)}, u32[]{:S(2)}) collective-permute-start(bf16[256,1024]{0,1:T(8,128)(2,1)} %get-tuple-element.106), channel_id=1, source_target_pairs={{0,8},{8,0},{16,24},{24,16},{1,9},{9,1},{17,25},{25,17},{2,10},{10... | collective-permute-start | bytes 1572872 | tf_op jit(solution)/shard_map/ppermute | solution.py:478
  262.8 15.4 %collective-permute-start.9 = (bf16[128,1024]{1,0:T(8,128)(2,1)}, bf16[128,1024]{1,0:T(8,128)(2,1)}, u32[]{:S(2)}, u32[]{:S(2)}) collective-permute-start(bf16[128,1024]{1,0:T(8,128)(2,1)} %slice.511), channel_id=1, source_target_pairs={{0,8},{8,0},{16,24},{24,16},{1,9},{9,1},{17,25},{25,17},{2,10},{10... | collective-permute-start | bytes 786440 | tf_op jit(solution)/shard_map/ppermute | solution.py:478
  267.9 15.9 %collective-permute-start.10 = (bf16[256,1024]{1,0:T(8,128)(2,1)}, bf16[256,1024]{1,0:T(8,128)(2,1)}, u32[]{:S(2)}, u32[]{:S(2)}) collective-permute-start(bf16[256,1024]{1,0:T(8,128)(2,1)} %get-tuple-element.108), channel_id=1, source_target_pairs={{0,8},{8,0},{16,24},{24,16},{1,9},{9,1},{17,25},{25,17},{2,10},{10... | collective-permute-start | bytes 1572872 | tf_op jit(solution)/shard_map/ppermute | solution.py:478
  285.8 10.7 %collective-permute-start.11 = (bf16[128,1024]{1,0:T(8,128)(2,1)}, bf16[128,1024]{1,0:T(8,128)(2,1)}, u32[]{:S(2)}, u32[]{:S(2)}) collective-permute-start(bf16[128,1024]{1,0:T(8,128)(2,1)} %slice.515), channel_id=1, source_target_pairs={{0,16},{8,24},{16,0},{24,8},{1,17},{9,25},{17,1},{25,9},{2,18},{10... | collective-permute-start | bytes 786440 | tf_op jit(solution)/shard_map/ppermute | solution.py:478
  308.6 10.3 %collective-permute-start.22 = (bf16[256,512]{1,0:T(8,128)(2,1)S(1)}, bf16[256,512]{1,0:T(8,128)(2,1)S(1)}, u32[]{:S(2)}, u32[]{:S(2)}) collective-permute-start(bf16[256,512]{1,0:T(8,128)(2,1)S(1)} %pad_maximum_fusion.28), channel_id=1, source_target_pairs={{0,24},{8,16},{16,8},{24,0},{1,25},{9,17},{17,9},{25,1},{2,26},{10... | collective-permute-start | bytes 786440 | tf_op jit(solution)/shard_map/ppermute | solution.py:478
  355.3 180.7 %reduce-scatter.6.cloned.1.call-start = ((), (), s32[]{:S(2)}) async-start(), calls=%async_computation.14 | async-start | bytes 4718592 | tf_op jit(solution)/shard_map/reduce_scatter | solution.py:924
  370.6 15.0 %collective-permute-start.23 = (bf16[256,1024]{0,1:T(8,128)(2,1)S(1)}, bf16[256,1024]{0,1:T(8,128)(2,1)}, u32[]{:S(2)}, u32[]{:S(2)}) collective-permute-start(bf16[256,1024]{0,1:T(8,128)(2,1)S(1)} %slice.540), channel_id=1, source_target_pairs={{0,16},{8,24},{16,0},{24,8},{1,17},{9,25},{17,1},{25,9},{2,18},{10... | collective-permute-start | bytes 1572872 | tf_op jit(solution)/shard_map/ppermute | solution.py:478
  371.5 35.9 %all-to-all-start.2 = ((bf16[8,32,1024]{2,1,0:T(8,128)(2,1)}), bf16[8,32,1024]{2,1,0:T(8,128)(2,1)}, u32[]{:S(2)}, u32[]{:S(2)}) async-start(bf16[8,32,1024]{2,1,0:T(8,128)(2,1)} %get-tuple-element.122), calls=%async_computation.2 | async-start | bytes 1048576 | tf_op jit(solution)/shard_map/all_to_all | solution.py:541
  387.8 15.0 %collective-permute-start.25 = (bf16[256,1024]{0,1:T(8,128)(2,1)}, bf16[256,1024]{0,1:T(8,128)(2,1)}, u32[]{:S(2)}, u32[]{:S(2)}) collective-permute-start(bf16[256,1024]{0,1:T(8,128)(2,1)} %get-tuple-element.104), channel_id=1, source_target_pairs={{0,8},{8,0},{16,24},{24,16},{1,9},{9,1},{17,25},{25,17},{2,10},{10... | collective-permute-start | bytes 1572872 | tf_op jit(solution)/shard_map/ppermute | solution.py:478
  394.9 16.7 %collective-permute-start.24 = (bf16[128,1024]{0,1:T(8,128)(2,1)}, bf16[128,1024]{0,1:T(8,128)(2,1)S(1)}, u32[]{:S(2)}, u32[]{:S(2)}) collective-permute-start(bf16[128,1024]{0,1:T(8,128)(2,1)} %slice.542), channel_id=1, source_target_pairs={{0,8},{8,0},{16,24},{24,16},{1,9},{9,1},{17,25},{25,17},{2,10},{10... | collective-permute-start | bytes 786440 | tf_op jit(solution)/shard_map/ppermute | solution.py:478
  407.4 12.8 %all-to-all-start.3 = ((bf16[4,2,32,1024]{3,2,1,0:T(8,128)(2,1)}), bf16[4,2,32,1024]{3,2,1,0:T(8,128)(2,1)}, u32[]{:S(2)}, u32[]{:S(2)}) async-start(bf16[4,2,32,1024]{3,2,1,0:T(8,128)(2,1)} %bitcast.25), calls=%async_computation.3 | async-start | bytes 1048576 | tf_op jit(solution)/shard_map/all_to_all | solution.py:543
  420.2 31.2 %all-to-all-start.6 = ((bf16[8,32,1024]{2,1,0:T(8,128)(2,1)}), bf16[8,32,1024]{2,1,0:T(8,128)(2,1)}, u32[]{:S(2)}, u32[]{:S(2)}) async-start(bf16[8,32,1024]{2,1,0:T(8,128)(2,1)} %bitcast.47), calls=%async_computation.6 | async-start | bytes 1048576 | tf_op jit(solution)/shard_map/all_to_all | solution.py:541
  434.1 65.4 %collective-permute-start.37 = (bf16[128,1024]{1,0:T(8,128)(2,1)S(1)}, bf16[128,1024]{1,0:T(8,128)(2,1)S(1)}, u32[]{:S(2)}, u32[]{:S(2)}) collective-permute-start(bf16[128,1024]{1,0:T(8,128)(2,1)S(1)} %pad_maximum_fusion.25), channel_id=1, source_target_pairs={{0,8},{8,0},{16,24},{24,16},{1,9},{9,1},{17,25},{25,17},{2,10},{10... | collective-permute-start | bytes 786440 | tf_op jit(solution)/shard_map/ppermute | solution.py:478
  451.4 53.4 %all-to-all-start.7 = ((bf16[4,2,32,1024]{3,2,1,0:T(8,128)(2,1)}), bf16[4,2,32,1024]{3,2,1,0:T(8,128)(2,1)S(1)}, u32[]{:S(2)}, u32[]{:S(2)}) async-start(bf16[4,2,32,1024]{3,2,1,0:T(8,128)(2,1)} %bitcast.48), calls=%async_computation.7 | async-start | bytes 1048576 | tf_op jit(solution)/shard_map/all_to_all | solution.py:543
  (72 other events, 566.6 us)
Sparse Core Ops, SparseCore 0:
  12.7 54.0 all-gather.3
  69.0 56.6 all-gather.5
  127.9 27.7 all-gather.7
  235.4 37.3 reduce-scatter.7
  355.5 49.7 reduce-scatter.9
  407.4 59.4 reduce-scatter.5
